TPU v7x, 32 devices: a whole 2x2x4 slice. The times are simulated.
32 devices in a mesh: dp: 4 (over y, x), seq: 8 (over z, core).
Axes of the slice: x: 2, y: 2, z: 4, core: 2. Of those that a mesh axis runs over, the one named last changes fastest.
Arguments:
- block_input: bfloat16 [4, 1536, 2560], P('dp', 'seq'), may hold values from -70 to 70
- qkv_weight: bfloat16 [2560, 1792], P(('dp', 'seq')), may hold values from -1 to 1
- out_weight: bfloat16 [2560, 1280], P(('dp', 'seq')), may hold values from -6 to 6
- ffn_weight: bfloat16 [2560, 7680], P(('dp', 'seq')), may hold values from -0.125 to 0.125
- down_weight: bfloat16 [2560, 3840], P(('dp', 'seq')), may hold values from -0.09375 to 0.09375
- attn_gain: bfloat16 [2560], P(('dp', 'seq')), may hold values from 0.099609375 to 1.8984375
- ffn_gain: bfloat16 [2560], P(('dp', 'seq')), may hold values from 0.099609375 to 1.8984375
- cotangent: bfloat16 [4, 1536, 2560], P('dp', 'seq'), may hold values from -6 to 6
Outputs:
- block_output: bfloat16 [4, 1536, 2560], P('dp', 'seq')
- grad_input: float32 [4, 1536, 2560], P('dp', 'seq')
- grad_qkv: float32 [2560, 1792], P(('dp', 'seq'))
- grad_out: float32 [2560, 1280], P(('dp', 'seq'))
- grad_ffn: float32 [2560, 7680], P(('dp', 'seq'))
- grad_down: float32 [2560, 3840], P(('dp', 'seq'))
- grad_attn_gain: float32 [2560], P(('dp', 'seq'))
- grad_ffn_gain: float32 [2560], P(('dp', 'seq'))
All inputs are finite; a program needn't handle non-finite values.
Results may differ from a plain program's by a relative error of at most 0.013.
The roundings to bfloat16 on the way count: a program that leaves them out, or rounds other values in their place, can miss the bound.
Values may be sent and summed in bfloat16 or wider, within the bound.
No kernel may reach another device: no remote copies, remote signals or barrier semaphores. Data moves between devices by JAX's collectives and lax.ppermute only.
A program may use at most 704 MiB of HBM per device.

v0:
```python
import jax
import jax.numpy as jnp
from jax import lax
from jax.sharding import PartitionSpec as P

HEADS = 5
HEAD = 256
FF = 3840
WINDOW = 2048
REACH = 11


EPSILON = 1e-06
GELU_C = 0.7978845608028654


def rope_tables(positions):
    half_dim = HEAD // 2
    frequency = 10000.0 ** (-jnp.arange(half_dim, dtype=jnp.float32) / half_dim)
    angles = positions.astype(jnp.float32)[:, None] * frequency[None, :]
    return (jnp.cos(angles), jnp.sin(angles))


def rotate(values, cosine, sine_part):
    half_dim = values.shape[-1] // 2
    first_half = values[..., :half_dim]
    second_half = values[..., half_dim:]
    return jnp.concatenate(
        [
            first_half * cosine - second_half * sine_part,
            second_half * cosine + first_half * sine_part,
        ],
        -1,
    )


def unrotate(values, cosine, sine_part):
    half_dim = values.shape[-1] // 2
    first_half = values[..., :half_dim]
    second_half = values[..., half_dim:]
    return jnp.concatenate(
        [
            first_half * cosine + second_half * sine_part,
            second_half * cosine - first_half * sine_part,
        ],
        -1,
    )


def gelu_parts(gate_in):
    cubic_term = 0.044715
    inner_arg = GELU_C * (gate_in + cubic_term * gate_in**3)
    tangent = jnp.tanh(inner_arg)
    gelu_value = 0.5 * gate_in * (1.0 + tangent)
    gelu_slope = 0.5 * (1.0 + tangent) + 0.5 * gate_in * (1.0 - tangent**2) * GELU_C * (
        1.0 + 3.0 * cubic_term * gate_in**2
    )
    return (gelu_value, gelu_slope)


def visible(query_pos, key_pos):
    later = query_pos[:, None] - key_pos[None, :]
    return (key_pos[None, :] >= 0) & (later >= 0) & (later < WINDOW)


def masked_scores(queries, keys_win, visible_mask):
    scores = jnp.einsum("qhd,kd->hqk", queries, keys_win, preferred_element_type=jnp.float32)
    return jnp.where(visible_mask[None], scores, -jnp.inf)


def attend(queries, keys_win, values_win, visible_mask):
    scores = masked_scores(queries, keys_win, visible_mask)
    row_peak = jnp.max(scores, -1, keepdims=True)
    log_total = row_peak + jnp.log(jnp.sum(jnp.exp(scores - row_peak), -1, keepdims=True))
    attn_probs = jnp.exp(scores - log_total).astype(jnp.bfloat16)
    attn_mixed = jnp.einsum(
        "hqk,kd->qhd", attn_probs, values_win, preferred_element_type=jnp.float32
    )
    return (attn_mixed.astype(jnp.bfloat16), log_total)


def attend_back(queries, keys_win, values_win, visible_mask, log_total, grad_mixed):
    attn_probs = jnp.exp(masked_scores(queries, keys_win, visible_mask) - log_total)
    grad_values = jnp.einsum(
        "hqk,qhd->kd",
        attn_probs.astype(jnp.bfloat16),
        grad_mixed,
        preferred_element_type=jnp.float32,
    )
    grad_probs = jnp.einsum(
        "qhd,kd->hqk", grad_mixed, values_win, preferred_element_type=jnp.float32
    )
    row_delta = jnp.sum(attn_probs * grad_probs, -1, keepdims=True)
    grad_scores = (attn_probs * (grad_probs - row_delta)).astype(jnp.bfloat16)
    grad_queries = jnp.einsum(
        "hqk,kd->qhd", grad_scores, keys_win, preferred_element_type=jnp.float32
    )
    grad_keys = jnp.einsum("hqk,qhd->kd", grad_scores, queries, preferred_element_type=jnp.float32)
    return (grad_queries, grad_keys, grad_values)


def contract_rows(left_rows, right_rows):
    return lax.dot_general(
        left_rows, right_rows, (((0,), (0,)), ((), ())), preferred_element_type=jnp.float32
    )


def contract_cols(left_rows, right_rows):
    return lax.dot_general(
        left_rows, right_rows, (((1,), (1,)), ((), ())), preferred_element_type=jnp.float32
    )


def sum_to_owners(lefts, rights, dp_count, seq_count, owned_rows):
    term = jnp.concatenate(
        [contract_rows(left_rows, right_rows) for left_rows, right_rows in zip(lefts, rights)], 1
    )
    columns = term.shape[1]
    pieces = term.reshape(dp_count * seq_count, owned_rows, columns)
    arrived = lax.all_to_all(pieces, ("dp", "seq"), split_axis=0, concat_axis=0, tiled=True)
    return jnp.sum(arrived, 0)


def body(
    block_input, qkv_weight, out_weight, ffn_weight, down_weight, attn_gain, ffn_gain, cotangent
):
    tokens = block_input[0]
    cot_rows = cotangent[0]
    rows_here = tokens.shape[0]
    owned_rows = qkv_weight.shape[0]
    seq_index = lax.axis_index("seq")
    seq_count = lax.axis_size("seq")
    dp_count = lax.axis_size("dp")
    width_q = HEADS * HEAD
    win_rows = (REACH + 1) * rows_here
    margin = REACH * rows_here
    query_scale = HEAD ** (-0.5)
    qkv_full, out_full, ffn_full, down_full, gain_one, gain_two = (
        lax.all_gather(qkv_weight, ("dp", "seq"), axis=0, tiled=True),
        lax.all_gather(out_weight, ("dp", "seq"), axis=0, tiled=True),
        lax.all_gather(ffn_weight, ("dp", "seq"), axis=0, tiled=True),
        lax.all_gather(down_weight, ("dp", "seq"), axis=0, tiled=True),
        lax.all_gather(attn_gain, ("dp", "seq"), axis=0, tiled=True),
        lax.all_gather(ffn_gain, ("dp", "seq"), axis=0, tiled=True),
    )
    gain_one = gain_one.astype(jnp.float32)
    gain_two = gain_two.astype(jnp.float32)
    positions = seq_index * rows_here + jnp.arange(rows_here, dtype=jnp.int32)
    cosine, sine_part = rope_tables(positions)
    token_f = tokens.astype(jnp.float32)
    inv_one = lax.rsqrt(jnp.mean(token_f * token_f, -1, keepdims=True) + EPSILON)
    normed_one = (token_f * inv_one * gain_one).astype(jnp.bfloat16)
    qkv_rows = jnp.dot(normed_one, qkv_full, preferred_element_type=jnp.float32)
    queries = (
        rotate(
            qkv_rows[:, :width_q].reshape(rows_here, HEADS, HEAD),
            cosine[:, None, :],
            sine_part[:, None, :],
        )
        * query_scale
    ).astype(jnp.bfloat16)
    keys_own = rotate(qkv_rows[:, width_q : width_q + HEAD], cosine, sine_part).astype(jnp.bfloat16)
    kv_rows = jnp.concatenate([keys_own, qkv_rows[:, width_q + HEAD :].astype(jnp.bfloat16)], -1)
    every_kv = lax.all_gather(kv_rows, "seq", axis=0, tiled=True)
    padded = jnp.concatenate([jnp.zeros((margin, 2 * HEAD), jnp.bfloat16), every_kv], 0)
    window_kv = lax.dynamic_slice_in_dim(padded, seq_index * rows_here, win_rows, 0)
    keys_win = window_kv[:, :HEAD]
    values_win = window_kv[:, HEAD:]
    key_pos = (seq_index - REACH) * rows_here + jnp.arange(win_rows, dtype=jnp.int32)
    visible_mask = visible(positions, key_pos)
    attn_mixed, log_total = attend(queries, keys_win, values_win, visible_mask)
    attn_flat = attn_mixed.reshape(rows_here, width_q)
    hidden_one = token_f + contract_cols(attn_flat, out_full)
    inv_two = lax.rsqrt(jnp.mean(hidden_one * hidden_one, -1, keepdims=True) + EPSILON)
    normed_two = (hidden_one * inv_two * gain_two).astype(jnp.bfloat16)
    gate_up = jnp.dot(normed_two, ffn_full, preferred_element_type=jnp.float32)
    gelu_value, gelu_slope = gelu_parts(gate_up[:, :FF])
    up_part = gate_up[:, FF:]
    hidden = (gelu_value * up_part).astype(jnp.bfloat16)
    output_rows = (hidden_one + contract_cols(hidden, down_full)).astype(jnp.bfloat16)
    grad_hidden = jnp.dot(cot_rows, down_full, preferred_element_type=jnp.float32)
    grad_gate_up = jnp.concatenate(
        [grad_hidden * up_part * gelu_slope, grad_hidden * gelu_value], -1
    ).astype(jnp.bfloat16)
    grad_norm_two = contract_cols(grad_gate_up, ffn_full)
    gain_two_grad = jnp.sum(grad_norm_two * hidden_one * inv_two, 0)
    scaled_two = gain_two * grad_norm_two
    grad_h_one = (
        cot_rows.astype(jnp.float32)
        + inv_two * scaled_two
        - hidden_one * inv_two**3 * jnp.mean(scaled_two * hidden_one, -1, keepdims=True)
    )
    grad_h_bf = grad_h_one.astype(jnp.bfloat16)
    grad_attn = (
        jnp.dot(grad_h_bf, out_full, preferred_element_type=jnp.float32)
        .astype(jnp.bfloat16)
        .reshape(rows_here, HEADS, HEAD)
    )
    grad_queries, grad_keys, grad_values = attend_back(
        queries, keys_win, values_win, visible_mask, log_total, grad_attn
    )
    grad_window = jnp.concatenate([grad_keys, grad_values], -1)
    spread = jnp.zeros((margin + rows_here * seq_count, 2 * HEAD), jnp.float32)
    spread = lax.dynamic_update_slice_in_dim(spread, grad_window, seq_index * rows_here, 0)
    own_grad = lax.psum_scatter(spread[margin:], "seq", scatter_dimension=0, tiled=True)
    grad_query = unrotate(grad_queries, cosine[:, None, :], sine_part[:, None, :]) * query_scale
    grad_key = unrotate(own_grad[:, :HEAD], cosine, sine_part)
    grad_qkv_rows = jnp.concatenate(
        [grad_query.reshape(rows_here, width_q), grad_key, own_grad[:, HEAD:]], -1
    ).astype(jnp.bfloat16)
    grad_norm_one = contract_cols(grad_qkv_rows, qkv_full)
    gain_one_grad = jnp.sum(grad_norm_one * token_f * inv_one, 0)
    scaled_one = gain_one * grad_norm_one
    grad_rows = (
        grad_h_one
        + inv_one * scaled_one
        - token_f * inv_one**3 * jnp.mean(scaled_one * token_f, -1, keepdims=True)
    )
    attn_sums = sum_to_owners(
        (normed_one, grad_h_bf), (grad_qkv_rows, attn_flat), dp_count, seq_count, owned_rows
    )
    ffn_sums = sum_to_owners(
        (normed_two, cot_rows), (grad_gate_up, hidden), dp_count, seq_count, owned_rows
    )
    gain_sums = (
        lax.psum_scatter(gain_one_grad, ("dp", "seq"), scatter_dimension=0, tiled=True),
        lax.psum_scatter(gain_two_grad, ("dp", "seq"), scatter_dimension=0, tiled=True),
    )
    edge_one = width_q + 2 * HEAD
    return (
        output_rows[None],
        grad_rows[None],
        attn_sums[:, :edge_one],
        attn_sums[:, edge_one:],
        ffn_sums[:, : 2 * FF],
        ffn_sums[:, 2 * FF :],
        gain_sums[0],
        gain_sums[1],
    )


def solution(mesh):
    placed = (
        P("dp", "seq", None),
        P(("dp", "seq"), None),
        P(("dp", "seq"), None),
        P(("dp", "seq"), None),
        P(("dp", "seq"), None),
        P(("dp", "seq")),
        P(("dp", "seq")),
        P("dp", "seq", None),
    )
    return jax.shard_map(
        body,
        mesh=mesh,
        in_specs=placed,
        out_specs=(
            P("dp", "seq", None),
            P("dp", "seq", None),
            P(("dp", "seq"), None),
            P(("dp", "seq"), None),
            P(("dp", "seq"), None),
            P(("dp", "seq"), None),
            P(("dp", "seq")),
            P(("dp", "seq")),
        ),
        check_vma=False,
    )
```

profile of v0, /device:TPU:0, one launch (start us, length us, event | category | flops | bytes accessed | tf_op | source)
XLA Modules:
  0.0 4015.1 jit_solution(6429920383393174742)
XLA Ops:
  9.7 42.9 %all-reduce.6 = (bf16[2560]{0:T(1024)(128)(2,1)S(1)}, bf16[2560]{0:T(1024)(128)(2,1)S(1)}) all-reduce(bf16[2560]{0:T(1024)(128)(2,1)S(1)} %dynamic-update-slice, bf16[2560]{0:T(1024)(128)(2,1)S(1)} %dynamic-update-slice.1), channel_id=1, replica_groups=mesh['dp'=4,'seq'=8] {'dp','seq'}, use_global_device_ids=true, to_apply=%add.1 | all-reduce | flops 5120 | bytes 20480
  54.6 40.2 %all-gather.6.cloned.1.call-done = bf16[2560,1792]{1,0:T(8,128)(2,1)} async-done(((bf16[80,1792]{1,0:T(8,128)(2,1)}), bf16[2560,1792]{1,0:T(8,128)(2,1)}) %all-gather.6.cloned.1.call-update) | async-done | bytes 9175056 | tf_op jit(solution)/shard_map/all_gather | solution.py:139
  108.2 18.8 all-gather.8.cloned.1.call-done
  136.2 63.2 %all-gather.10.cloned.1.call-done = bf16[2560,1280]{1,0:T(8,128)(2,1)} async-done(((bf16[80,1280]{1,0:T(8,128)(2,1)}), bf16[2560,1280]{1,0:T(8,128)(2,1)}) %all-gather.10.cloned.1.call-update) | async-done | bytes 6553616 | tf_op jit(solution)/shard_map/all_gather | solution.py:140
  204.8 217.9 %all-gather.12.cloned.1.call-done = bf16[2560,7680]{1,0:T(8,128)(2,1)} async-done(((bf16[80,7680]{1,0:T(8,128)(2,1)}), bf16[2560,7680]{1,0:T(8,128)(2,1)}) %all-gather.12.cloned.1.call-update) | async-done | bytes 39321616 | tf_op jit(solution)/shard_map/all_gather | solution.py:141
  422.7 19.9 fusion.88
  442.6 108.8 %all-gather.14.cloned.1.call-done = bf16[2560,3840]{1,0:T(8,128)(2,1)} async-done(((bf16[80,3840]{1,0:T(8,128)(2,1)}), bf16[2560,3840]{1,0:T(8,128)(2,1)}) %all-gather.14.cloned.1.call-update) | async-done | bytes 19660816 | tf_op jit(solution)/shard_map/all_gather | solution.py:142
  551.4 12.6 fusion.15
  564.0 21.6 multiply_reduce_fusion
  594.7 6.2 convolution_bitcast_fusion.1
  619.5 6.6 fusion.43
  626.2 25.4 reduce-scatter.2.cloned.1.call-done
  659.5 14.8 pad_maximum_fusion.1
  674.3 30.8 copy.51
  709.7 16.8 convolution_bitcast_fusion
  726.6 28.9 fusion.25
  755.4 77.5 %pad_maximum_fusion = f32[2560,11520]{1,0:T(8,128)} fusion(f32[2560,3840]{1,0:T(8,128)} %convolution_bitcast_fusion, f32[2560,7680]{1,0:T(8,128)} %fusion.25), kind=kLoop, calls=%fused_computation | loop fusion | flops 29491200 | bytes 235929600 | tf_op jit(solution)/shard_map/concatenate | solution.py:115
  832.9 555.9 %all-to-all-done = f32[32,80,3072]{2,1,0:T(8,128)} async-done(((f32[32,80,3072]{2,1,0:T(8,128)}), f32[32,80,3072]{2,1,0:T(8,128)}, u32[]{:S(2)}, u32[]{:S(2)}) %all-to-all-start) | async-done | bytes 31457312 | tf_op jit(solution)/shard_map/all_to_all | solution.py:120
  1388.8 6.1 all-to-all-start.1
  1395.0 11.8 fusion.6
  1406.9 8.3 fusion.24
  1415.2 2531.7 %all-reduce.5 = (f32[2560]{0:T(1024)S(1)}, f32[2560]{0:T(1024)S(1)}) all-reduce(f32[2560]{0:T(1024)S(1)} %get-tuple-element.10, f32[2560]{0:T(1024)S(1)} %copy-done.30), channel_id=3, replica_groups=mesh['dp'=4,'seq'=8] {'dp','seq'}, use_global_device_ids=true, to_apply=%region_11.12.clone | all-reduce | flops 5120 | bytes 40960
  3951.4 11.4 reduce_sum.96
  3964.4 37.9 reduce_sum.97
  (157 shorter events, 84.3 us)
Async XLA Ops:
  7.2 87.7 %all-gather.6.cloned.1.call-start = ((), (), s32[]{:S(2)}) async-start(), calls=%async_computation.3 | async-start | bytes 9461760 | tf_op jit(solution)/shard_map/all_gather | solution.py:139
  7.9 119.1 %all-gather.8.cloned.1.call-start = ((), (), s32[]{:S(2)}) async-start(), calls=%async_computation.4 | async-start | bytes 1769472 | tf_op jit(solution)/shard_map/all_gather | solution.py:164
  52.5 601.8 %copy-start.28 = (f32[2560]{0:T(1024)}, f32[2560]{0:T(1024)S(1)}, u32[]{:S(2)}) copy-start(f32[2560]{0:T(1024)S(1)} %convert_element_type.62) | copy-start | bytes 30724
  54.6 599.7 %copy-start.31 = (f32[192]{0:T(256)}, f32[192]{0:T(256)S(1)}, u32[]{:S(2)}) copy-start(f32[192]{0:T(256)S(1)} %get-tuple-element.34) | copy-start | bytes 2308
  103.0 96.3 %all-gather.10.cloned.1.call-start = ((), (), s32[]{:S(2)}) async-start(), calls=%async_computation.5 | async-start | bytes 6758400 | tf_op jit(solution)/shard_map/all_gather | solution.py:140
  103.8 318.9 %all-gather.12.cloned.1.call-start = ((), (), s32[]{:S(2)}) async-start(), calls=%async_computation.6 | async-start | bytes 40550400 | tf_op jit(solution)/shard_map/all_gather | solution.py:141
  104.4 447.0 %all-gather.14.cloned.1.call-start = ((), (), s32[]{:S(2)}) async-start(), calls=%async_computation.7 | async-start | bytes 20275200 | tf_op jit(solution)/shard_map/all_gather | solution.py:142
  104.9 546.6 %reduce-scatter.2.cloned.1.call-start = ((), (), s32[]{:S(2)}) async-start(), calls=%async_computation.8 | async-start | bytes 3538944 | tf_op jit(solution)/shard_map/reduce_scatter | solution.py:205
  108.2 21.3 copy-start.20
  108.2 21.3 copy-start.22
  133.0 66.3 %copy-start.5 = (bf16[1,192,2560]{2,1,0:T(8,128)(2,1)S(1)}, bf16[1,192,2560]{2,1,0:T(8,128)(2,1)}, u32[]{:S(2)}) copy-start(bf16[1,192,2560]{2,1,0:T(8,128)(2,1)} %param.8) | copy-start | bytes 2949124
  204.8 359.2 %copy-start.3 = (f32[192,2560]{1,0:T(8,128)}, f32[192,2560]{1,0:T(8,128)S(1)}, u32[]{:S(2)}) copy-start(f32[192,2560]{1,0:T(8,128)S(1)} %get-tuple-element.40) | copy-start | bytes 5898244
  422.7 128.7 %copy-start.9 = (bf16[1,192,2560]{2,1,0:T(8,128)(2,1)S(1)}, bf16[1,192,2560]{2,1,0:T(8,128)(2,1)}, u32[]{:S(2)}) copy-start(bf16[1,192,2560]{2,1,0:T(8,128)(2,1)} %param.15) | copy-start | bytes 2949124
  588.5 31.0 copy-start.1
  588.5 12.4 slice-start
  705.1 683.7 %all-to-all-start = ((f32[32,80,3072]{2,1,0:T(8,128)}), f32[32,80,3072]{2,1,0:T(8,128)}, u32[]{:S(2)}, u32[]{:S(2)}) async-start(f32[32,80,3072]{2,1,0:T(8,128)} %bitcast.91), calls=%async_computation.1 | async-start | bytes 62914560 | tf_op jit(solution)/shard_map/all_to_all | solution.py:120
  709.7 16.9 copy-start.4
  1388.8 2575.6 %all-to-all-start.1 = ((f32[32,80,11520]{2,1,0:T(8,128)}), f32[32,80,11520]{2,1,0:T(8,128)}, u32[]{:S(2)}, u32[]{:S(2)}) async-start(f32[32,80,11520]{2,1,0:T(8,128)} %bitcast.19), calls=%async_computation.2 | async-start | bytes 235929600 | tf_op jit(solution)/shard_map/all_to_all | solution.py:120
  1394.9 11.9 copy-start.6
  1395.0 11.8 copy-start.12
  1395.0 11.8 copy-start.19
  1395.0 11.8 copy-start.25
  1406.9 2541.2 %copy-start.2 = (f32[192,2560]{1,0:T(8,128)S(1)}, f32[192,2560]{1,0:T(8,128)}, u32[]{:S(2)}) copy-start(f32[192,2560]{1,0:T(8,128)} %copy-done.1) | copy-start | bytes 5898244
  1406.9 2541.2 %copy-start.33 = (f32[192]{0:T(256)S(1)}, f32[192]{0:T(256)}, u32[]{:S(2)}) copy-start(f32[192]{0:T(256)} %get-tuple-element.33) | copy-start | bytes 2308
  (25 other events, 137.0 us)
Sparse Core Ops, SparseCore 0:
  10.8 83.9 all-gather.5
  103.2 23.7 all-gather.7
  129.8 69.4 all-gather.9
  202.2 220.4 all-gather.11
  425.6 125.7 all-gather.13
  612.9 38.6 reduce-scatter.1
where the time goes:
time: 4020 us
  blocking collectives  2570 us (64%)
  waiting for transfers between devices  1030 us (26%)
  matrix products  166 us (4%)
  other arithmetic  159 us (4%)
  local copies, waits for them, and re-layouts  56.2 us (1%)
    unnamed x2, blocking collectives  2570 us
    all_to_all x2, waiting for transfers between devices, sum_to_owners(): lax.all_to_all(pieces, ('dp', 'seq'), split_axis=0, concat_axis=0, tiled=...  556 us
    all_gather x1, waiting for transfers between devices, body(): lax.all_gather(ffn_weight, ('dp', 'seq'), axis=0, tiled=True)  218 us
    all_gather x1, waiting for transfers between devices, body(): lax.all_gather(down_weight, ('dp', 'seq'), axis=0, tiled=True)  109 us
    concatenate x2, other arithmetic, sum_to_owners(): jnp.concatenate([contract_rows(left_rows, right_rows) for left_rows, righ...  92.3 us
  transfers between devices with their start and end apart: 8, of which 7 were waited for; matrix products, arithmetic and copies ran while one was open for 5% of the time, Pallas kernels for 0%

commit v1 on v0

v1 whole, which is shorter than its diff:
```python
import jax
import jax.numpy as jnp
from jax import lax
from jax.experimental import pallas as pl
from jax.experimental.pallas import tpu as pltpu
from jax.sharding import Mesh, PartitionSpec as P


HEADS = 5
HEAD = 256
FF = 3840
WINDOW = 2048


EPSILON = 1e-06
GELU_C = 0.7978845608028654
CORES = 2
EVERY = ("da", "db", "z", "core")
SEQ = ("z", "core")
PAIR = ("da", "db")
PLANE = ("da", "db", "core")
LANES = 128
BF = jnp.bfloat16
F32 = jnp.float32


def rope_tables(positions):
    half_dim = HEAD // 2
    frequency = 10000.0 ** (-jnp.arange(half_dim, dtype=jnp.float32) / half_dim)
    angles = positions.astype(jnp.float32)[:, None] * frequency[None, :]
    return (jnp.cos(angles), jnp.sin(angles))


def rotate(values, cosine, sine_part):
    half_dim = values.shape[-1] // 2
    first_half = values[..., :half_dim]
    second_half = values[..., half_dim:]
    return jnp.concatenate(
        [
            first_half * cosine - second_half * sine_part,
            second_half * cosine + first_half * sine_part,
        ],
        -1,
    )


def unrotate(values, cosine, sine_part):
    half_dim = values.shape[-1] // 2
    first_half = values[..., :half_dim]
    second_half = values[..., half_dim:]
    return jnp.concatenate(
        [
            first_half * cosine + second_half * sine_part,
            second_half * cosine - first_half * sine_part,
        ],
        -1,
    )


def gelu_parts(gate_in):
    cubic_term = 0.044715
    inner_arg = GELU_C * (gate_in + cubic_term * gate_in**3)
    tangent = jnp.tanh(inner_arg)
    gelu_value = 0.5 * gate_in * (1.0 + tangent)
    gelu_slope = 0.5 * (1.0 + tangent) + 0.5 * gate_in * (1.0 - tangent**2) * GELU_C * (
        1.0 + 3.0 * cubic_term * gate_in**2
    )
    return (gelu_value, gelu_slope)


def contract_rows(left_rows, right_rows):
    return lax.dot_general(
        left_rows, right_rows, (((0,), (0,)), ((), ())), preferred_element_type=jnp.float32
    )


def contract_cols(left_rows, right_rows):
    return lax.dot_general(
        left_rows, right_rows, (((1,), (1,)), ((), ())), preferred_element_type=jnp.float32
    )


def gather(values, axes, axis=0, tiled=True):
    return lax.all_gather(values, axes, axis=axis, tiled=tiled)


def scatter(values, axes, axis=0):
    return lax.psum_scatter(values, axes, scatter_dimension=axis, tiled=True)


def exchange(values, axes):
    return lax.all_to_all(values, axes, split_axis=0, concat_axis=0, tiled=True)


def shift(values, axis, step):
    count = lax.axis_size(axis)
    return lax.ppermute(values, axis, [(i, (i + step) % count) for i in range(count)])


def slide(values, axis, step):
    count = lax.axis_size(axis)
    pairs = [(i, i + step) for i in range(count) if 0 <= i + step < count]
    return lax.ppermute(values, axis, pairs)


def pick(values, index, axis):
    return lax.dynamic_index_in_dim(values, index, axis, keepdims=False)


def line_gather(values, axis):
    count = lax.axis_size(axis)
    here = lax.axis_index(axis)
    right, left = values, values
    rights, lefts = [], []
    for _ in range(1, count):
        right = slide(right, axis, 1)
        left = slide(left, axis, -1)
        rights.append(right)
        lefts.append(left)
    pieces = [values]
    for k in range(1, count):
        pieces.append(jnp.where(here >= k, rights[k - 1], lefts[count - k - 1]))
    return pieces


def place(pieces, here, dim):
    count = len(pieces)
    shape = list(pieces[0].shape)
    shape.insert(dim, count)
    buffer = jnp.zeros(shape, pieces[0].dtype)
    for k, piece in enumerate(pieces):
        at = [0] * len(shape)
        at[dim] = (here - k) % count
        buffer = lax.dynamic_update_slice(buffer, jnp.expand_dims(piece, dim), at)
    return buffer


def reduce_axis(values, axis, dim):
    count = lax.axis_size(axis)
    here = lax.axis_index(axis)
    total = pick(values, here, dim).astype(F32)
    for k in range(1, count):
        piece = pick(values, (here + k) % count, dim).astype(BF)
        piece = shift(piece, axis, k)
        total = total + piece.astype(F32)
    return total


def reduce_plane(values, cut):
    half = values.shape[cut] // 2
    first, second = (lax.slice_in_dim(values, i * half, (i + 1) * half, axis=cut) for i in (0, 1))
    first = reduce_axis(reduce_axis(first, "db", 1), "da", 0)
    second = reduce_axis(reduce_axis(second, "da", 0), "db", 0)
    return jnp.concatenate([first, second], cut - 2)


def reduce_rows(term, owned_rows, cut):
    count_a, count_b, count_z = (lax.axis_size(axis) for axis in ("da", "db", "z"))
    columns = term.shape[1]
    blocks = term.reshape(count_a, count_b, CORES, count_z * owned_rows, columns)
    paired = reduce_axis(blocks, "core", 2)
    plane = reduce_plane(paired.astype(BF), cut)
    return reduce_axis(plane.reshape(count_z, owned_rows, columns), "z", 0)


def reduce_tokens(own, other, rows_here, cut):
    count_a, count_b = (lax.axis_size(axis) for axis in PAIR)
    width = own.shape[1]
    other = shift(other, "core", 1)
    paired = (own.astype(F32) + other.astype(F32)).astype(BF)
    return reduce_plane(paired.reshape(count_a, count_b, rows_here, width), cut)


def plane_gather(values):
    count_a, count_b = (lax.axis_size(axis) for axis in PAIR)
    count = count_a * count_b
    here_a, here_b, core = (lax.axis_index(axis) for axis in PLANE)
    rows, width = values.shape
    buffer = jnp.zeros((count_a, count_b, CORES, rows, width), values.dtype)
    for ka in range(count_a):
        for kb in range(count_b):
            piece = values
            if ka or kb:
                pairs = [
                    (
                        i,
                        (i // count_b + ka) % count_a * count_b + (i % count_b + kb) % count_b,
                    )
                    for i in range(count)
                ]
                piece = lax.ppermute(values, PAIR, pairs)
            other = shift(piece, "core", 1)
            at_a, at_b = (here_a - ka) % count_a, (here_b - kb) % count_b
            for part, at in ((piece, core), (other, 1 - core)):
                buffer = lax.dynamic_update_slice(
                    buffer, part[None, None, None], (at_a, at_b, at, 0, 0)
                )
    return buffer.reshape(count * CORES * rows, width)


def hidden_cuts(total, group, part):
    return [
        (min(j * part, total), max(0, min(part, total - j * part))) for j in range(group)
    ]


def pack_shares(ffn_weight, down_weight, group, part):
    rows, total = down_weight.shape
    cuts = hidden_cuts(total, group, part)

    def kernel(ffn_ref, down_ref, out_ref):
        for j, (first, count) in enumerate(cuts):
            if count < part:
                out_ref[j] = jnp.zeros((rows, 3 * part), BF)
            if count:
                out_ref[j, :, pl.ds(0, count)] = ffn_ref[:, pl.ds(first, count)]
                out_ref[j, :, pl.ds(part, count)] = ffn_ref[:, pl.ds(total + first, count)]
                out_ref[j, :, pl.ds(2 * part, count)] = down_ref[:, pl.ds(first, count)]

    return pl.pallas_call(
        kernel,
        out_shape=jax.ShapeDtypeStruct((group, rows, 3 * part), BF),
        name="pack_shares",
    )(ffn_weight, down_weight)


def unpack_gate_up(summed, ffn_weight, ffn_gain, group, part):
    rows, double = ffn_weight.shape
    total = double // 2
    cuts = hidden_cuts(total, group, part)

    def kernel(sum_ref, weight_ref, gain_ref, out_ref, gain_out_ref):
        gain_sum = jnp.zeros((rows, 1), F32)
        for j, (first, count) in enumerate(cuts):
            if count:
                for source, target in ((0, first), (part, total + first)):
                    piece = sum_ref[j, :, pl.ds(source, count)].astype(F32)
                    out_ref[:, pl.ds(target, count)] = piece
                    weight = weight_ref[:, pl.ds(target, count)].astype(F32)
                    gain_sum = gain_sum + jnp.sum(piece * weight, 1, keepdims=True)
        gain_out_ref[...] = gain_sum / gain_ref[...].astype(F32)

    return pl.pallas_call(
        kernel,
        out_shape=(
            jax.ShapeDtypeStruct((rows, double), F32),
            jax.ShapeDtypeStruct((rows, 1), F32),
        ),
        name="unpack_gate_up",
    )(summed, ffn_weight, ffn_gain[:, None])


def unpack_down(summed, total, group, part):
    rows = summed.shape[1]
    cuts = hidden_cuts(total, group, part)

    def kernel(sum_ref, out_ref):
        for j, (first, count) in enumerate(cuts):
            if count:
                out_ref[:, pl.ds(first, count)] = sum_ref[j, :, pl.ds(0, count)].astype(F32)

    return pl.pallas_call(
        kernel, out_shape=jax.ShapeDtypeStruct((rows, total), F32), name="unpack_down"
    )(summed)


def reorder(values, dp_count, first_count, second_count, addend=None, kind=None):
    rows, width = values.shape
    owned = width // (dp_count * first_count * second_count)
    kind = kind or values.dtype

    def kernel(*refs):
        out_ref = refs[-1]
        for d in range(dp_count):
            for i in range(first_count):
                for j in range(second_count):
                    source = pl.ds(((d * first_count + i) * second_count + j) * owned, owned)
                    target = pl.ds(((d * second_count + j) * first_count + i) * owned, owned)
                    piece = refs[0][:, source]
                    if addend is not None:
                        piece = piece + refs[1][:, source]
                    out_ref[:, target] = piece.astype(kind)

    operands = (values,) if addend is None else (values, addend)
    return pl.pallas_call(
        kernel, out_shape=jax.ShapeDtypeStruct((rows, width), kind), name="reorder"
    )(*operands)


def attend(rows_in, kv_pieces, cosine, sine_part, query_pos, key_pos):
    rows = rows_in.shape[0]
    query_scale = HEAD ** (-0.5)
    count = len(kv_pieces)
    length = count * rows

    def kernel(*refs):
        kv_refs = refs[:count]
        q_ref, cos_ref, sin_ref, qp_ref, kp_ref, out_ref, lse_ref, qr_ref, kv_all = refs[count:]
        for i, ref in enumerate(kv_refs):
            kv_all[pl.ds(i * rows, rows), :] = ref[...]
        later = qp_ref[...] - kp_ref[...]
        seen = (later >= 0) & (later < WINDOW)
        lanes = lax.broadcasted_iota(jnp.int32, (rows, LANES), 1)
        totals = jnp.zeros((rows, LANES), F32)
        for h in range(HEADS):
            at = pl.ds(h * HEAD, HEAD)
            rotated = rotate(q_ref[:, at], cos_ref[...], sin_ref[...])
            query = (rotated * query_scale).astype(BF)
            qr_ref[:, at] = query
            scores = jnp.where(seen, contract_cols(query, kv_all[:, :HEAD]), -jnp.inf)
            peak = jnp.max(scores, -1, keepdims=True)
            weights = jnp.exp(scores - peak)
            total = jnp.sum(weights, -1, keepdims=True)
            probs = (weights * (1.0 / total)).astype(BF)
            mixed = jnp.dot(probs, kv_all[:, HEAD:], preferred_element_type=F32)
            out_ref[:, at] = mixed.astype(BF)
            totals = jnp.where(lanes == h, peak + jnp.log(total), totals)
        lse_ref[...] = totals

    return pl.pallas_call(
        kernel,
        out_shape=(
            jax.ShapeDtypeStruct((rows, HEADS * HEAD), BF),
            jax.ShapeDtypeStruct((rows, LANES), F32),
            jax.ShapeDtypeStruct((rows, HEADS * HEAD), BF),
        ),
        scratch_shapes=[pltpu.VMEM((length, 2 * HEAD), BF)],
        cost_estimate=pl.CostEstimate(
            flops=4 * rows * length * HEADS * HEAD,
            transcendentals=rows * length * HEADS,
            bytes_accessed=4 * length * HEAD + 10 * rows * HEADS * HEAD,
        ),
        name="attend",
    )(*kv_pieces, rows_in, cosine, sine_part, query_pos, key_pos)


def attend_back(queries, kv_pieces, cosine, sine_part, query_pos, key_pos, totals, grad_mixed):
    rows = queries.shape[0]
    count = len(kv_pieces)
    length = count * rows
    half = length // 2
    query_scale = HEAD ** (-0.5)

    def kernel(*refs):
        kv_refs = refs[:count]
        q_ref, cos_ref, sin_ref, qp_ref, kp_ref, lse_ref, do_ref = refs[count : count + 7]
        dq_ref, own_ref, other_ref, kv_all, ds_all, probs_all, q_all, do_all = refs[count + 7 :]
        for i, ref in enumerate(kv_refs):
            kv_all[pl.ds(i * rows, rows), :] = ref[...]
        later = qp_ref[...] - kp_ref[...]
        seen = (later >= 0) & (later < WINDOW)
        for h in range(HEADS):
            at = pl.ds(h * HEAD, HEAD)
            below = pl.ds(h * rows, rows)
            query = q_ref[:, at]
            grad_out = do_ref[:, at]
            scores = jnp.where(seen, contract_cols(query, kv_all[:, :HEAD]), -jnp.inf)
            probs = jnp.exp(scores - lse_ref[:, h : h + 1])
            grad_probs = contract_cols(grad_out, kv_all[:, HEAD:])
            delta = jnp.sum(probs * grad_probs, -1, keepdims=True)
            grad_scores = (probs * (grad_probs - delta)).astype(BF)
            ds_all[below, :] = grad_scores
            probs_all[below, :] = probs.astype(BF)
            q_all[below, :] = query
            do_all[below, :] = grad_out
            grad_query = jnp.dot(grad_scores, kv_all[:, :HEAD], preferred_element_type=F32)
            grad_query = unrotate(grad_query, cos_ref[...], sin_ref[...]) * query_scale
            dq_ref[:, at] = grad_query.astype(BF)
        for ref, first, kind in ((own_ref, 0, F32), (other_ref, half, BF)):
            part = pl.ds(first, half)
            ref[:, :HEAD] = contract_rows(ds_all[:, part], q_all[...]).astype(kind)
            ref[:, HEAD:] = contract_rows(probs_all[:, part], do_all[...]).astype(kind)

    stacked = HEADS * rows
    return pl.pallas_call(
        kernel,
        out_shape=(
            jax.ShapeDtypeStruct((rows, HEADS * HEAD), BF),
            jax.ShapeDtypeStruct((half, 2 * HEAD), F32),
            jax.ShapeDtypeStruct((half, 2 * HEAD), BF),
        ),
        scratch_shapes=[
            pltpu.VMEM((length, 2 * HEAD), BF),
            pltpu.VMEM((stacked, length), BF),
            pltpu.VMEM((stacked, length), BF),
            pltpu.VMEM((stacked, HEAD), BF),
            pltpu.VMEM((stacked, HEAD), BF),
        ],
        cost_estimate=pl.CostEstimate(
            flops=10 * rows * length * HEADS * HEAD,
            transcendentals=rows * length * HEADS,
            bytes_accessed=7 * length * HEAD + 10 * rows * HEADS * HEAD,
        ),
        name="attend_back",
    )(*kv_pieces, queries, cosine, sine_part, query_pos, key_pos, totals, grad_mixed)


def plane_specs(dp_count, rows_here):
    together = 2
    steps = dp_count // together

    def tokens(columns):
        return pl.BlockSpec(
            (together, 1, rows_here, columns),
            lambda i, core: (i % steps, jnp.where(i < steps, 1 - core[0], core[0]), 0, 0),
        )

    def halves(columns):
        rows = together * rows_here
        return (
            pl.BlockSpec((rows, columns), lambda i, core: (jnp.minimum(i, steps - 1), 0)),
            pl.BlockSpec((rows, columns), lambda i, core: (jnp.maximum(i - steps, 0), 0)),
        )

    return steps, together * rows_here, tokens, halves


def feed_forward(core, tokens_in, weight, grad_hidden):
    dp_count, _, rows_here, width = tokens_in.shape
    part = grad_hidden.shape[3]
    steps, rows, tokens, halves = plane_specs(dp_count, rows_here)

    def kernel(core_ref, in_ref, weight_ref, grad_ref, hid_ref, dgu_ref, other_ref, own_ref):
        step = pl.program_id(0)
        both = jnp.dot(in_ref[...].reshape(rows, width), weight_ref[...], preferred_element_type=F32)
        gelu_value, gelu_slope = gelu_parts(both[:, :part])
        up_part = both[:, part:]
        grad = grad_ref[...].reshape(rows, part)
        hid_ref[...] = (gelu_value * up_part).astype(BF).reshape(hid_ref.shape)
        dgu = jnp.concatenate([grad * up_part * gelu_slope, grad * gelu_value], 1).astype(BF)
        dgu_ref[...] = dgu.reshape(dgu_ref.shape)
        term = contract_cols(dgu, weight_ref[...]).astype(BF)

        @pl.when(step < steps)
        def _():
            other_ref[...] = term

        @pl.when(step >= steps)
        def _():
            own_ref[...] = term

    count = dp_count * CORES * rows_here
    half = jax.ShapeDtypeStruct((count // 2, width), BF)
    return pl.pallas_call(
        kernel,
        grid_spec=pltpu.PrefetchScalarGridSpec(
            num_scalar_prefetch=1,
            grid=(2 * steps,),
            in_specs=[
                tokens(width),
                pl.BlockSpec((width, 2 * part), lambda i, core: (0, 0)),
                tokens(part),
            ],
            out_specs=(tokens(part), tokens(2 * part), *halves(width)),
        ),
        out_shape=(
            jax.ShapeDtypeStruct((dp_count, CORES, rows_here, part), BF),
            jax.ShapeDtypeStruct((dp_count, CORES, rows_here, 2 * part), BF),
            half,
            half,
        ),
        cost_estimate=pl.CostEstimate(
            flops=8 * count * width * part,
            transcendentals=count * part,
            bytes_accessed=4 * count * width + 4 * width * part + 10 * count * part,
        ),
        name="feed_forward",
    )(core, tokens_in, weight, grad_hidden)


def down_product(core, hidden, weight):
    dp_count, _, rows_here, part = hidden.shape
    width = weight.shape[0]
    steps, rows, tokens, halves = plane_specs(dp_count, rows_here)

    def kernel(core_ref, in_ref, weight_ref, other_ref, own_ref):
        step = pl.program_id(0)
        term = contract_cols(in_ref[...].reshape(rows, part), weight_ref[...]).astype(BF)

        @pl.when(step < steps)
        def _():
            other_ref[...] = term

        @pl.when(step >= steps)
        def _():
            own_ref[...] = term

    count = dp_count * CORES * rows_here
    half = jax.ShapeDtypeStruct((count // 2, width), BF)
    return pl.pallas_call(
        kernel,
        grid_spec=pltpu.PrefetchScalarGridSpec(
            num_scalar_prefetch=1,
            grid=(2 * steps,),
            in_specs=[tokens(part), pl.BlockSpec((width, part), lambda i, core: (0, 0))],
            out_specs=halves(width),
        ),
        out_shape=(half, half),
        cost_estimate=pl.CostEstimate(
            flops=2 * count * width * part,
            transcendentals=0,
            bytes_accessed=2 * count * (width + part) + 2 * width * part,
        ),
        name="down_product",
    )(core, hidden, weight)


def weight_term(left, right, dp_count, z_count):
    tokens, width = left.shape
    columns = right.shape[1]
    per_dp = width // dp_count
    owned = per_dp // (z_count * CORES)
    together = 1
    while (together * per_dp) % LANES:
        together *= 2
    block = together * per_dp

    def kernel(left_ref, right_ref, out_ref):
        term = contract_rows(left_ref[...], right_ref[...]).astype(BF)
        for d in range(together):
            for c in range(CORES):
                for z in range(z_count):
                    first = d * per_dp + (c * z_count + z) * owned
                    out_ref[z, d, c] = term[first : first + owned]

    return pl.pallas_call(
        kernel,
        grid=(width // block,),
        in_specs=[
            pl.BlockSpec((tokens, block), lambda i: (0, i)),
            pl.BlockSpec((tokens, columns), lambda i: (0, 0)),
        ],
        out_specs=pl.BlockSpec(
            (z_count, together, CORES, owned, columns), lambda i: (0, i, 0, 0, 0)
        ),
        out_shape=jax.ShapeDtypeStruct((z_count, dp_count, CORES, owned, columns), BF),
        cost_estimate=pl.CostEstimate(
            flops=2 * tokens * width * columns,
            transcendentals=0,
            bytes_accessed=2 * (tokens * width + tokens * columns + width * columns),
        ),
        name="weight_term",
    )(left, right)


def body(
    block_input, qkv_weight, out_weight, ffn_weight, down_weight, attn_gain, ffn_gain, cotangent
):
    tokens = block_input[0]
    cot_rows = cotangent[0]
    rows_here, width = tokens.shape
    owned_rows = qkv_weight.shape[0]
    dp_count = lax.axis_size("da") * lax.axis_size("db")
    z_count = lax.axis_size("z")
    z_index = lax.axis_index("z")
    core = lax.axis_index("core")
    group = dp_count * CORES
    width_q = HEADS * HEAD
    width_qkv = width_q + 2 * HEAD
    part = -(-FF // (LANES * group)) * LANES

    tokens = reorder(tokens, dp_count, z_count, CORES)
    cot_rows = reorder(cot_rows, dp_count, z_count, CORES)

    gain_columns = jnp.stack([attn_gain, ffn_gain], 1)
    gain_columns = jnp.pad(gain_columns, ((0, 0), (0, LANES - 2)))
    qkv_line = gather(jnp.concatenate([qkv_weight, gain_columns], 1), "z")
    packed = pack_shares(ffn_weight, down_weight, group, part)
    mine = exchange(packed, PLANE)
    qkv_line, mine, out_weight = lax.optimization_barrier((qkv_line, mine, out_weight))
    share = group // 2
    gate_up_w = jnp.zeros((group, z_count, owned_rows, 2 * part), BF)
    down_w = jnp.zeros((group, z_count, owned_rows, part), BF)
    for i in range(2):
        pieces = line_gather(mine[i * share : (i + 1) * share, None], "z")
        for k, piece in enumerate(pieces):
            at = (i * share, (z_index - k) % z_count, 0, 0)
            gate_up_w = lax.dynamic_update_slice(gate_up_w, piece[..., : 2 * part], at)
            down_w = lax.dynamic_update_slice(down_w, piece[..., 2 * part :], at)
    gate_up_w = gate_up_w.reshape(width, 2 * part)
    down_w = down_w.reshape(width, part)
    qkv_gain = gather(qkv_line, PLANE)
    qkv_full = qkv_gain[:, :width_qkv]
    gain_one = qkv_gain[:, width_qkv].astype(F32)
    gain_two = qkv_gain[:, width_qkv + 1].astype(F32)
    out_pieces = [out_weight] + [shift(out_weight, "z", k) for k in range(1, z_count)]
    out_line = place(out_pieces, z_index, 0).reshape(z_count * owned_rows, width_q)
    out_full = plane_gather(out_line)
    cot_plane = plane_gather(cot_rows)

    positions = (z_index * CORES + core) * rows_here + jnp.arange(rows_here, dtype=jnp.int32)
    cosine, sine_part = rope_tables(positions)
    token_f = tokens.astype(jnp.float32)
    inv_one = lax.rsqrt(jnp.mean(token_f * token_f, -1, keepdims=True) + EPSILON)
    normed_one = (token_f * inv_one * gain_one).astype(jnp.bfloat16)
    qkv_rows = jnp.dot(normed_one, qkv_full, preferred_element_type=jnp.float32)
    keys_own = rotate(qkv_rows[:, width_q : width_q + HEAD], cosine, sine_part).astype(jnp.bfloat16)
    kv_rows = jnp.concatenate([keys_own, qkv_rows[:, width_q + HEAD :].astype(jnp.bfloat16)], -1)
    kv_pieces = [kv_rows] + [shift(kv_rows, "z", k) for k in range(1, z_count)]
    kv_pieces = kv_pieces + [shift(piece, "core", 1) for piece in kv_pieces]
    block_z = (z_index - jnp.arange(z_count, dtype=jnp.int32)) % z_count
    block_at = jnp.concatenate([block_z * CORES + core, block_z * CORES + (1 - core)])
    key_pos = (
        block_at[:, None] * rows_here + jnp.arange(rows_here, dtype=jnp.int32)[None, :]
    ).reshape(1, -1)
    query_pos = positions[:, None]
    attn_flat, log_total, queries = attend(
        qkv_rows, kv_pieces, cosine, sine_part, query_pos, key_pos
    )
    hidden_one = token_f + contract_cols(attn_flat, out_full)
    inv_two = lax.rsqrt(jnp.mean(hidden_one * hidden_one, -1, keepdims=True) + EPSILON)
    normed_two = (hidden_one * inv_two * gain_two).astype(jnp.bfloat16)

    normed_plane = gather(normed_two, PLANE)
    grad_hidden = jnp.dot(cot_plane, down_w, preferred_element_type=jnp.float32)
    core_at = jnp.full((1,), core, jnp.int32)
    in_blocks = (dp_count, CORES, rows_here, -1)
    hidden, grad_gate_up, dn2_other, dn2_own = feed_forward(
        core_at, normed_plane.reshape(in_blocks), gate_up_w, grad_hidden.reshape(in_blocks)
    )
    grad_norm_two = reduce_tokens(dn2_own, dn2_other, rows_here, 2)
    down_other, down_own = down_product(core_at, hidden, down_w)
    down_rows = reduce_tokens(down_own, down_other, rows_here, 3)
    output_rows = reorder(hidden_one, dp_count, CORES, z_count, down_rows, BF)

    def sum_ffn(left, right):
        right = right.reshape(left.shape[0], -1)
        term = weight_term(left, right, dp_count, z_count).reshape(width, right.shape[1])
        mine = scatter(term, "z").reshape(group, owned_rows, right.shape[1])
        return exchange(mine, PLANE)

    gate_up_sum = sum_ffn(normed_plane, grad_gate_up)
    down_sum = sum_ffn(cot_plane, hidden)
    grad_ffn, gain_two_grad = unpack_gate_up(gate_up_sum, ffn_weight, ffn_gain, group, part)
    gain_two_grad = gain_two_grad[:, 0]
    grad_down = unpack_down(down_sum, FF, group, part)

    scaled_two = gain_two * grad_norm_two
    grad_h_one = (
        cot_rows.astype(jnp.float32)
        + inv_two * scaled_two
        - hidden_one * inv_two**3 * jnp.mean(scaled_two * hidden_one, -1, keepdims=True)
    )
    grad_h_bf = grad_h_one.astype(jnp.bfloat16)
    grad_attn = jnp.dot(grad_h_bf, out_full, preferred_element_type=F32).astype(BF)
    grad_query, kv_own, kv_other = attend_back(
        queries, kv_pieces, cosine, sine_part, query_pos, key_pos, log_total, grad_attn
    )
    kv_other = shift(kv_other, "core", 1)
    paired = (kv_own + kv_other.astype(F32)).reshape(z_count, rows_here, 2 * HEAD)
    own_grad = paired[0]
    for k in range(1, z_count):
        piece = paired[k].astype(BF)
        piece = shift(piece, "z", -k)
        own_grad = own_grad + piece.astype(F32)
    grad_key = unrotate(own_grad[:, :HEAD], cosine, sine_part)
    grad_kv = jnp.concatenate([grad_key, own_grad[:, HEAD:]], -1).astype(BF)

    gout_term = contract_rows(grad_h_bf, attn_flat).astype(BF)
    gq_term = contract_rows(normed_one, grad_query).astype(BF)
    gkv_term = contract_rows(normed_one, grad_kv).astype(BF)
    late_kv = grad_kv + 0.0 * gkv_term[0, 0]
    grad_norm_one = contract_cols(jnp.concatenate([grad_query, late_kv], -1), qkv_full)
    scaled_one = gain_one * grad_norm_one
    grad_rows = (
        grad_h_one
        + inv_one * scaled_one
        - token_f * inv_one**3 * jnp.mean(scaled_one * token_f, -1, keepdims=True)
    )
    grad_rows = reorder(grad_rows, dp_count, CORES, z_count)

    grad_out = reduce_rows(gout_term, owned_rows, 3)
    grad_qkv = jnp.concatenate(
        [reduce_rows(gq_term, owned_rows, 2), reduce_rows(gkv_term, owned_rows, 2)],
        1,
    )
    gain_one_grad = jnp.sum(grad_qkv * qkv_weight.astype(F32), 1) / attn_gain.astype(F32)
    return (
        output_rows[None],
        grad_rows[None],
        grad_qkv,
        grad_out,
        grad_ffn,
        grad_down,
        gain_one_grad,
        gain_two_grad,
    )


def solution(mesh):
    dp_count = mesh.shape["dp"]
    seq_count = mesh.shape["seq"]
    split = Mesh(mesh.devices.reshape(dp_count // 2, 2, seq_count // CORES, CORES), EVERY)
    by_token = P(PAIR, SEQ, None)
    by_row = P(EVERY, None)
    by_gain = P(EVERY)


    return jax.shard_map(
        body,
        mesh=split,
        in_specs=(by_token, by_row, by_row, by_row, by_row, by_gain, by_gain, by_token),
        out_specs=(by_token, by_token, by_row, by_row, by_row, by_row, by_gain, by_gain),
        check_vma=False,
    )
```

time: 4020 us -> 718 us (0.18)
  blocking collectives: 2570 us -> 30.5 us
  waiting for transfers between devices: 1030 us -> 319 us
  matrix products: 166 us -> 36.8 us
  other arithmetic: 159 us -> 44.6 us
  starting transfers between devices: 11.1 us -> 112 us
  Pallas kernels: 0 us -> 93.1 us
    unnamed x2 -> x0, blocking collectives: 2570 us -> none
    all_to_all x2, waiting for transfers between devices: 556 us -> 0.01 us  [exchange(): return lax.all_to_all(values, axes, split_axis=0, concat_axis=0, tiled=True)]
    all_gather x5 -> x3, waiting for transfers between devices: 449 us -> 9.55 us  [gather(): return lax.all_gather(values, axes, axis=axis, tiled=tiled)]
    ppermute x0 -> x74, waiting for transfers between devices: none -> 310 us  [the longest x56 161 us: shift(): lax.ppermute(values, axis, [(i, (i + step) % count) for i in range(count)])]
    ppermute x0 -> x74, starting transfers between devices: none -> 103 us  [the longest x56 57.2 us: shift(): lax.ppermute(values, axis, [(i, (i + step) % count) for i in range(count)])]
    pallas_call x0 -> x13, Pallas kernels: none -> 93.1 us  [the longest x1 24.4 us: feed_forward(): pl.pallas_call(kernel, grid_spec=pltpu.PrefetchScalarGridSpec(num_scalar_...]
    concatenate x2 -> x5, other arithmetic: 92.3 us -> 3.45 us  [the longest x4 1.75 us: reduce_plane(): return jnp.concatenate([first, second], cut - 2)]
    dot_general x4 -> x3, matrix products: 56.6 us -> 6.24 us  [contract_rows(): lax.dot_general(left_rows, right_rows, (((0,), (0,)), ((), ())), preferre...]
  transfers between devices with their start and end apart: 8 -> 81, of which waited for: 7 -> 36; matrix products, arithmetic and copies ran while one was open for 5% -> 18% of each run, Pallas kernels for 0% -> 8%
where the time goes in v1:
time: 718 us; the launch traced here: 709 us
  waiting for transfers between devices  319 us (44%)
  starting transfers between devices  112 us (16%)
  Pallas kernels  93.1 us (13%)
  local copies, waits for them, and re-layouts  56.9 us (8%)
  other arithmetic  44.6 us (6%)
  matrix products  36.8 us (5%)
  blocking collectives  30.5 us (4%)
  between operations  16 us (2%)
    ppermute x56, waiting for transfers between devices, shift(): lax.ppermute(values, axis, [(i, (i + step) % count) for i in range(count)])  161 us
    ppermute x12, waiting for transfers between devices, slide(): return lax.ppermute(values, axis, pairs)  86.6 us
    ppermute x6, waiting for transfers between devices, plane_gather(): piece = lax.ppermute(values, PAIR, pairs)  61.9 us
    ppermute x56, starting transfers between devices, shift(): lax.ppermute(values, axis, [(i, (i + step) % count) for i in range(count)])  57.2 us
    ppermute x12, starting transfers between devices, slide(): return lax.ppermute(values, axis, pairs)  37.5 us
    all_to_all x1, blocking collectives, exchange(): return lax.all_to_all(values, axes, split_axis=0, concat_axis=0, tiled=True)  30.5 us
    pallas_call x1, Pallas kernels, feed_forward(): pl.pallas_call(kernel, grid_spec=pltpu.PrefetchScalarGridSpec(num_scalar_...  24.4 us
    pallas_call x2, Pallas kernels, weight_term(): pl.pallas_call(kernel, grid=(width // block,), in_specs=[pl.BlockSpec((to...  21 us
  transfers between devices with their start and end apart: 81, of which 36 were waited for; matrix products, arithmetic and copies ran while one was open for 18% of the time, Pallas kernels for 8%

profile of v1, /device:TPU:0, one launch (start us, length us, event | category | flops | bytes accessed | tf_op | source)
XLA Modules:
  0.0 708.9 jit_solution(6914013718880210281)
XLA Ops:
  12.6 30.5 %all_to_all.15 = bf16[8,80,1536]{2,1,0:T(8,128)(2,1)} all-to-all(bf16[8,80,1536]{2,1,0:T(8,128)(2,1)} %pack_shares.1), channel_id=1, replica_groups=mesh['da'=2,'db'=2,'z'=4,'core'=2] {'da','db','core'}, dimensions={0} | all-to-all | bytes 3932160 | tf_op jit(solution)/shard_map/all_to_all | solution.py:92
  83.1 32.1 %collective-permute-done.11 = bf16[320,1280]{1,0:T(8,128)(2,1)S(1)} collective-permute-done((bf16[320,1280]{1,0:T(8,128)(2,1)S(1)}, bf16[320,1280]{1,0:T(8,128)(2,1)S(1)}, u32[]{:S(2)}, u32[]{:S(2)}) %collective-permute-start.11) | collective-permute-done | bytes 819232 | tf_op jit(solution)/shard_map/ppermute | solution.py:191
  115.7 29.8 %collective-permute-done.15 = bf16[320,1280]{1,0:T(8,128)(2,1)S(1)} collective-permute-done((bf16[320,1280]{1,0:T(8,128)(2,1)S(1)}, bf16[320,1280]{1,0:T(8,128)(2,1)S(1)}, u32[]{:S(2)}, u32[]{:S(2)}) %collective-permute-start.15) | collective-permute-done | bytes 819232 | tf_op jit(solution)/shard_map/ppermute | solution.py:191
  150.3 8.7 %all-gather.6.cloned.1.call-done = bf16[2560,1920]{1,0:T(8,128)(2,1)} async-done(((bf16[320,1920]{1,0:T(8,128)(2,1)}), bf16[2560,1920]{1,0:T(8,128)(2,1)}) %all-gather.6.cloned.1.call-update) | async-done | bytes 9830416 | tf_op jit(solution)/shard_map/all_gather | solution.py:84
  179.7 8.0 %collective-permute-done.1.refs_2_ = bf16[192,512]{1,0:T(8,128)(2,1)S(1)} collective-permute-done((bf16[192,512]{1,0:T(8,128)(2,1)S(1)}, bf16[192,512]{1,0:T(8,128)(2,1)S(1)}, u32[]{:S(2)}, u32[]{:S(2)}) %collective-permute-start.1) | collective-permute-done | bytes 196640 | tf_op jit(solution)/shard_map/ppermute | solution.py:97
  246.2 15.2 %collective-permute-done.24 = bf16[4,1,80,1536]{3,2,0,1:T(8,128)(2,1)S(1)} collective-permute-done((bf16[4,1,80,1536]{3,2,0,1:T(8,128)(2,1)S(1)}, bf16[4,1,80,1536]{3,2,0,1:T(8,128)(2,1)S(1)}, u32[]{:S(2)}, u32[]{:S(2)}) %collective-permute-start.24) | collective-permute-done | bytes 983072 | tf_op jit(solution)/shard_map/ppermute | solution.py:103
  268.7 13.7 %collective-permute-done.19 = bf16[4,1,80,1536]{3,2,0,1:T(8,128)(2,1)S(1)} collective-permute-done((bf16[4,1,80,1536]{3,2,0,1:T(8,128)(2,1)S(1)}, bf16[4,1,80,1536]{3,2,0,1:T(8,128)(2,1)S(1)}, u32[]{:S(2)}, u32[]{:S(2)}) %collective-permute-start.19) | collective-permute-done | bytes 983072 | tf_op jit(solution)/shard_map/ppermute | solution.py:103
  288.3 15.2 %collective-permute-done.25 = bf16[4,1,80,1536]{3,2,0,1:T(8,128)(2,1)S(1)} collective-permute-done((bf16[4,1,80,1536]{3,2,0,1:T(8,128)(2,1)S(1)}, bf16[4,1,80,1536]{3,2,0,1:T(8,128)(2,1)S(1)}, u32[]{:S(2)}, u32[]{:S(2)}) %collective-permute-start.25) | collective-permute-done | bytes 983072 | tf_op jit(solution)/shard_map/ppermute | solution.py:103
  309.8 14.7 %collective-permute-done.20 = bf16[4,1,80,1536]{3,2,0,1:T(8,128)(2,1)S(1)} collective-permute-done((bf16[4,1,80,1536]{3,2,0,1:T(8,128)(2,1)S(1)}, bf16[4,1,80,1536]{3,2,0,1:T(8,128)(2,1)S(1)}, u32[]{:S(2)}, u32[]{:S(2)}) %collective-permute-start.20) | collective-permute-done | bytes 983072 | tf_op jit(solution)/shard_map/ppermute | solution.py:103
  326.2 18.8 %collective-permute-done.26 = bf16[4,1,80,1536]{3,2,0,1:T(8,128)(2,1)S(1)} collective-permute-done((bf16[4,1,80,1536]{3,2,0,1:T(8,128)(2,1)S(1)}, bf16[4,1,80,1536]{3,2,0,1:T(8,128)(2,1)S(1)}, u32[]{:S(2)}, u32[]{:S(2)}) %collective-permute-start.26) | collective-permute-done | bytes 983072 | tf_op jit(solution)/shard_map/ppermute | solution.py:103
  358.9 24.4 %feed_forward.1 = (bf16[4,2,192,512]{3,2,1,0:T(8,128)(2,1)}, bf16[4,2,192,1024]{3,2,1,0:T(8,128)(2,1)}, bf16[768,2560]{1,0:T(8,128)(2,1)}, bf16[768,2560]{1,0:T(8,128)(2,1)}) custom-call(s32[1]{0:T(128)} %bitcast.17.core_ref, bf16[4,2,192,2560]{3,2,1,0:T(8,128)(2,1)} %bitcast.335, bf16[2560,1024]{1,0:T(8,128)(2,1)} %bitcast.29.weight_ref, ...), custom_call_target="tpu_custom_call" | custom-call | flops 16106127360 | bytes 28835840 | tf_op jit(solution)/shard_map/feed_forward/pallas_call | solution.py:444
  383.3 8.5 %weight_term.3 = bf16[4,4,2,80,512]{4,3,2,1,0:T(8,128)(2,1)} custom-call(bf16[1536,2560]{1,0:T(8,128)(2,1)} %bitcast.309, bf16[1536,512]{1,0:T(8,128)(2,1)} %bitcast.338), custom_call_target="tpu_custom_call" | custom-call | flops 4026531840 | bytes 12058624 | tf_op jit(solution)/shard_map/weight_term/pallas_call | solution.py:526
  392.4 9.7 %down_product.1 = (bf16[768,2560]{1,0:T(8,128)(2,1)}, bf16[768,2560]{1,0:T(8,128)(2,1)}) custom-call(s32[1]{0:T(128)} %bitcast.17.core_ref, bf16[4,2,192,512]{3,2,1,0:T(8,128)(2,1)} %get-tuple-element.29.in_ref, bf16[2560,512]{1,0:T(8,128)(2,1)} %bitcast.324), custom_call_target="tpu_custom_call" | custom-call | flops 4026531840 | bytes 12058624 | tf_op jit(solution)/shard_map/down_product/pallas_call | solution.py:490
  403.2 12.5 %weight_term.2 = bf16[4,4,2,80,1024]{4,3,2,1,0:T(8,128)(2,1)} custom-call(bf16[1536,2560]{1,0:T(8,128)(2,1)} %all-gather.8.cloned.1.call-done.left_ref, bf16[1536,1024]{1,0:T(8,128)(2,1)} %bitcast.337), custom_call_target="tpu_custom_call" | custom-call | flops 8053063680 | bytes 16252928 | tf_op jit(solution)/shard_map/weight_term/pallas_call | solution.py:526
  428.5 16.7 %collective-permute-done.42 = bf16[2,96,2560]{2,1,0:T(8,128)(2,1)S(1)} collective-permute-done((bf16[2,96,2560]{2,1,0:T(8,128)(2,1)S(1)}, bf16[2,96,2560]{2,1,0:T(8,128)(2,1)S(1)}, u32[]{:S(2)}, u32[]{:S(2)}) %collective-permute-start.42) | collective-permute-done | bytes 983072 | tf_op jit(solution)/shard_map/ppermute | solution.py:97
  449.6 16.7 %collective-permute-done.37 = bf16[2,192,1280]{2,1,0:T(8,128)(2,1)S(1)} collective-permute-done((bf16[2,192,1280]{2,1,0:T(8,128)(2,1)S(1)}, bf16[2,192,1280]{2,1,0:T(8,128)(2,1)S(1)}, u32[]{:S(2)}, u32[]{:S(2)}) %collective-permute-start.37) | collective-permute-done | bytes 983072 | tf_op jit(solution)/shard_map/ppermute | solution.py:97
  484.3 7.6 %convolution_convert_fusion.3.refs_14_ = bf16[192,1280]{1,0:T(8,128)(2,1)} fusion(bf16[2560,1280]{1,0:T(8,128)(2,1)} %bitcast.16, f32[192,2560]{1,0:T(8,128)S(1)} %multiply_subtract_fusion), kind=kOutput, calls=%fused_computation.23 | convolution fusion | flops 1259028480 | bytes 9011200 | tf_op jit(solution)/shard_map/dot_general | solution.py:645
  493.8 8.8 %attend_back.1 = (bf16[192,1280]{1,0:T(8,128)(2,1)}, f32[768,512]{1,0:T(8,128)}, bf16[768,512]{1,0:T(8,128)(2,1)}) custom-call(bf16[192,512]{1,0:T(8,128)(2,1)} %copy-done.28, bf16[192,512]{1,0:T(8,128)(2,1)} %copy-done.32, bf16[192,512]{1,0:T(8,128)(2,1)} %copy-done.33, bf16[192,512]{1,0:T(8,128)(2,1)} %copy-done.34, bf16[192,512]{1,0:T(8,128)(2,1)} %copy-done.35, ...), custom_call_target="tpu_custom_call" | custom-call | flops 3774873600 | bytes 5210112 | tf_op jit(solution)/shard_map/attend_back/pallas_call | solution.py:375
  518.8 9.3 %collective-permute-done.47 = bf16[192,512]{1,0:T(8,128)(2,1)S(1)} collective-permute-done((bf16[192,512]{1,0:T(8,128)(2,1)S(1)}, bf16[192,512]{1,0:T(8,128)(2,1)S(1)}, u32[]{:S(2)}, u32[]{:S(2)}) %collective-permute-start.47) | collective-permute-done | bytes 196640 | tf_op jit(solution)/shard_map/ppermute | solution.py:97
  528.0 25.0 %collective-permute-done.48 = bf16[192,512]{1,0:T(8,128)(2,1)S(1)} collective-permute-done((bf16[192,512]{1,0:T(8,128)(2,1)S(1)}, bf16[192,512]{1,0:T(8,128)(2,1)S(1)}, u32[]{:S(2)}, u32[]{:S(2)}) %collective-permute-start.48) | collective-permute-done | bytes 196640 | tf_op jit(solution)/shard_map/ppermute | solution.py:97
  614.6 13.6 %collective-permute-done.67 = bf16[2,320,640]{2,1,0:T(8,128)(2,1)S(1)} collective-permute-done((bf16[2,320,640]{2,1,0:T(8,128)(2,1)S(1)}, bf16[2,320,640]{2,1,0:T(8,128)(2,1)S(1)}, u32[]{:S(2)}, u32[]{:S(2)}) %collective-permute-start.67) | collective-permute-done | bytes 819232 | tf_op jit(solution)/shard_map/ppermute | solution.py:97
  630.9 14.8 %collective-permute-done.51 = bf16[2,160,1280]{2,1,0:T(8,128)(2,1)S(1)} collective-permute-done((bf16[2,160,1280]{2,1,0:T(8,128)(2,1)S(1)}, bf16[2,160,1280]{2,1,0:T(8,128)(2,1)S(1)}, u32[]{:S(2)}, u32[]{:S(2)}) %collective-permute-start.51) | collective-permute-done | bytes 819232 | tf_op jit(solution)/shard_map/ppermute | solution.py:97
  648.5 12.4 %collective-permute-done.52 = bf16[160,1280]{1,0:T(8,128)(2,1)S(1)} collective-permute-done((bf16[160,1280]{1,0:T(8,128)(2,1)S(1)}, bf16[160,1280]{1,0:T(8,128)(2,1)S(1)}, u32[]{:S(2)}, u32[]{:S(2)}) %collective-permute-start.52) | collective-permute-done | bytes 409632 | tf_op jit(solution)/shard_map/ppermute | solution.py:97
  685.3 8.9 %collective-permute-done.72 = bf16[80,1280]{1,0:T(8,128)(2,1)} collective-permute-done((bf16[80,1280]{1,0:T(8,128)(2,1)}, bf16[80,1280]{1,0:T(8,128)(2,1)}, u32[]{:S(2)}, u32[]{:S(2)}) %collective-permute-start.72) | collective-permute-done | bytes 204832 | tf_op jit(solution)/shard_map/ppermute | solution.py:97
  (395 shorter events, 317.3 us)
Async XLA Ops:
  9.7 149.3 %all-gather.6.cloned.1.call-start = ((), (), s32[]{:S(2)}) async-start(), calls=%async_computation.6 | async-start | bytes 11059200 | tf_op jit(solution)/shard_map/all_gather | solution.py:84
  44.0 314.9 %all-gather.8.cloned.1.call-start = ((), (), s32[]{:S(2)}) async-start(), calls=%async_computation.7 | async-start | bytes 8847360 | tf_op jit(solution)/shard_map/all_gather | solution.py:84
  46.9 127.5 %collective-permute-start.30 = (bf16[192,2560]{1,0:T(8,128)(2,1)}, bf16[192,2560]{1,0:T(8,128)(2,1)}, u32[]{:S(2)}, u32[]{:S(2)}) collective-permute-start(bf16[192,2560]{1,0:T(8,128)(2,1)} %reorder.5), channel_id=1, source_target_pairs={{0,8},{8,0},{16,24},{24,16},{1,9},{9,1},{17,25},{25,17},{2,10},{10... | collective-permute-start | bytes 2949128 | tf_op jit(solution)/shard_map/ppermute | solution.py:191
  71.0 44.1 %collective-permute-start.11 = (bf16[320,1280]{1,0:T(8,128)(2,1)S(1)}, bf16[320,1280]{1,0:T(8,128)(2,1)S(1)}, u32[]{:S(2)}, u32[]{:S(2)}) collective-permute-start(bf16[320,1280]{1,0:T(8,128)(2,1)S(1)} %bitcast.316), channel_id=1, source_target_pairs={{0,8},{8,0},{16,24},{24,16},{1,9},{9,1},{17,25},{25,17},{2,10},{10... | collective-permute-start | bytes 2457608 | tf_op jit(solution)/shard_map/ppermute | solution.py:191
  71.7 43.5 %collective-permute-start.13 = (bf16[320,1280]{1,0:T(8,128)(2,1)S(1)}, bf16[320,1280]{1,0:T(8,128)(2,1)S(1)}, u32[]{:S(2)}, u32[]{:S(2)}) collective-permute-start(bf16[320,1280]{1,0:T(8,128)(2,1)S(1)} %bitcast.317), channel_id=1, source_target_pairs={{0,16},{8,24},{16,0},{24,8},{1,17},{9,25},{17,1},{25,9},{2,18},{10... | collective-permute-start | bytes 2457608 | tf_op jit(solution)/shard_map/ppermute | solution.py:191
  73.0 72.5 %collective-permute-start.15 = (bf16[320,1280]{1,0:T(8,128)(2,1)S(1)}, bf16[320,1280]{1,0:T(8,128)(2,1)S(1)}, u32[]{:S(2)}, u32[]{:S(2)}) collective-permute-start(bf16[320,1280]{1,0:T(8,128)(2,1)S(1)} %bitcast.318), channel_id=1, source_target_pairs={{0,24},{8,16},{16,8},{24,0},{1,25},{9,17},{17,9},{25,1},{2,26},{10... | collective-permute-start | bytes 2457608 | tf_op jit(solution)/shard_map/ppermute | solution.py:191
  81.6 107.6 %collective-permute-start.32 = (bf16[192,2560]{1,0:T(8,128)(2,1)}, bf16[192,2560]{1,0:T(8,128)(2,1)}, u32[]{:S(2)}, u32[]{:S(2)}) collective-permute-start(bf16[192,2560]{1,0:T(8,128)(2,1)} %reorder.5), channel_id=1, source_target_pairs={{0,16},{8,24},{16,0},{24,8},{1,17},{9,25},{17,1},{25,9},{2,18},{10... | collective-permute-start | bytes 2949128 | tf_op jit(solution)/shard_map/ppermute | solution.py:191
  191.2 41.6 %collective-permute-start.33 = (bf16[192,2560]{1,0:T(8,128)(2,1)}, bf16[192,2560]{1,0:T(8,128)(2,1)}, u32[]{:S(2)}, u32[]{:S(2)}) collective-permute-start(bf16[192,2560]{1,0:T(8,128)(2,1)} %collective-permute-done.32), channel_id=1, source_target_pairs={{0,1},{1,0},{2,3},{3,2},{4,5},{5,4},{6,7},{7,6},{8,9},{9,8},{10,11... | collective-permute-start | bytes 2949128 | tf_op jit(solution)/shard_map/ppermute | solution.py:97
  206.4 264.6 %reduce-scatter.5.cloned.1.call-start = ((), (), s32[]{:S(2)}) async-start(), calls=%async_computation.9 | async-start | bytes 3276800 | tf_op jit(solution)/shard_map/reduce_scatter | solution.py:88
  240.3 42.1 %collective-permute-start.19 = (bf16[4,1,80,1536]{3,2,0,1:T(8,128)(2,1)S(1)}, bf16[4,1,80,1536]{3,2,0,1:T(8,128)(2,1)S(1)}, u32[]{:S(2)}, u32[]{:S(2)}) collective-permute-start(bf16[4,1,80,1536]{3,2,0,1:T(8,128)(2,1)S(1)} %collective-permute-done.18), channel_id=1, source_target_pairs={{2,0},{4,2},{6,4},{3,1},{5,3},{7,5},{10,8},{12,10},{14,12},{11,9},... | collective-permute-start | bytes 2949128 | tf_op jit(solution)/shard_map/ppermute | solution.py:103
  241.7 42.1 %collective-permute-start.21 = (bf16[4,1,80,1536]{3,2,0,1:T(8,128)(2,1)S(1)}, bf16[4,1,80,1536]{3,2,0,1:T(8,128)(2,1)S(1)}, u32[]{:S(2)}, u32[]{:S(2)}) collective-permute-start(bf16[4,1,80,1536]{3,2,0,1:T(8,128)(2,1)S(1)} %collective-permute-done.17), channel_id=1, source_target_pairs={{0,2},{2,4},{4,6},{1,3},{3,5},{5,7},{8,10},{10,12},{12,14},{9,11},... | collective-permute-start | bytes 2949128 | tf_op jit(solution)/shard_map/ppermute | solution.py:103
  261.3 42.1 %collective-permute-start.25 = (bf16[4,1,80,1536]{3,2,0,1:T(8,128)(2,1)S(1)}, bf16[4,1,80,1536]{3,2,0,1:T(8,128)(2,1)S(1)}, u32[]{:S(2)}, u32[]{:S(2)}) collective-permute-start(bf16[4,1,80,1536]{3,2,0,1:T(8,128)(2,1)S(1)} %collective-permute-done.24), channel_id=1, source_target_pairs={{2,0},{4,2},{6,4},{3,1},{5,3},{7,5},{10,8},{12,10},{14,12},{11,9},... | collective-permute-start | bytes 2949128 | tf_op jit(solution)/shard_map/ppermute | solution.py:103
  262.8 42.1 %collective-permute-start.27 = (bf16[4,1,80,1536]{3,2,0,1:T(8,128)(2,1)S(1)}, bf16[4,1,80,1536]{3,2,0,1:T(8,128)(2,1)S(1)}, u32[]{:S(2)}, u32[]{:S(2)}) collective-permute-start(bf16[4,1,80,1536]{3,2,0,1:T(8,128)(2,1)S(1)} %collective-permute-done.23), channel_id=1, source_target_pairs={{0,2},{2,4},{4,6},{1,3},{3,5},{5,7},{8,10},{10,12},{12,14},{9,11},... | collective-permute-start | bytes 2949128 | tf_op jit(solution)/shard_map/ppermute | solution.py:103
  282.4 42.1 %collective-permute-start.20 = (bf16[4,1,80,1536]{3,2,0,1:T(8,128)(2,1)S(1)}, bf16[4,1,80,1536]{3,2,0,1:T(8,128)(2,1)S(1)}, u32[]{:S(2)}, u32[]{:S(2)}) collective-permute-start(bf16[4,1,80,1536]{3,2,0,1:T(8,128)(2,1)S(1)} %collective-permute-done.19), channel_id=1, source_target_pairs={{2,0},{4,2},{6,4},{3,1},{5,3},{7,5},{10,8},{12,10},{14,12},{11,9},... | collective-permute-start | bytes 2949128 | tf_op jit(solution)/shard_map/ppermute | solution.py:103
  283.9 42.1 %collective-permute-start.22 = (bf16[4,1,80,1536]{3,2,0,1:T(8,128)(2,1)S(1)}, bf16[4,1,80,1536]{3,2,0,1:T(8,128)(2,1)S(1)}, u32[]{:S(2)}, u32[]{:S(2)}) collective-permute-start(bf16[4,1,80,1536]{3,2,0,1:T(8,128)(2,1)S(1)} %collective-permute-done.21), channel_id=1, source_target_pairs={{0,2},{2,4},{4,6},{1,3},{3,5},{5,7},{8,10},{10,12},{12,14},{9,11},... | collective-permute-start | bytes 2949128 | tf_op jit(solution)/shard_map/ppermute | solution.py:103
  303.5 41.5 %collective-permute-start.26 = (bf16[4,1,80,1536]{3,2,0,1:T(8,128)(2,1)S(1)}, bf16[4,1,80,1536]{3,2,0,1:T(8,128)(2,1)S(1)}, u32[]{:S(2)}, u32[]{:S(2)}) collective-permute-start(bf16[4,1,80,1536]{3,2,0,1:T(8,128)(2,1)S(1)} %collective-permute-done.25), channel_id=1, source_target_pairs={{2,0},{4,2},{6,4},{3,1},{5,3},{7,5},{10,8},{12,10},{14,12},{11,9},... | collective-permute-start | bytes 2949128 | tf_op jit(solution)/shard_map/ppermute | solution.py:103
  304.9 41.2 %collective-permute-start.28 = (bf16[4,1,80,1536]{3,2,0,1:T(8,128)(2,1)S(1)}, bf16[4,1,80,1536]{3,2,0,1:T(8,128)(2,1)S(1)}, u32[]{:S(2)}, u32[]{:S(2)}) collective-permute-start(bf16[4,1,80,1536]{3,2,0,1:T(8,128)(2,1)S(1)} %collective-permute-done.27), channel_id=1, source_target_pairs={{0,2},{2,4},{4,6},{1,3},{3,5},{5,7},{8,10},{10,12},{12,14},{9,11},... | collective-permute-start | bytes 2949128 | tf_op jit(solution)/shard_map/ppermute | solution.py:103
  391.8 278.4 %reduce-scatter.3.cloned.1.call-start = ((), (), s32[]{:S(2)}) async-start(), calls=%async_computation.8 | async-start | bytes 6553600 | tf_op jit(solution)/shard_map/reduce_scatter | solution.py:88
  427.3 41.1 %collective-permute-start.39 = (bf16[2,192,1280]{2,1,0:T(8,128)(2,1)S(1)}, bf16[2,192,1280]{2,1,0:T(8,128)(2,1)S(1)}, u32[]{:S(2)}, u32[]{:S(2)}) collective-permute-start(bf16[2,192,1280]{2,1,0:T(8,128)(2,1)S(1)} %dynamic-slice_bitcast_fusion.5), channel_id=1, source_target_pairs={{0,16},{16,0},{1,17},{17,1},{2,18},{18,2},{3,19},{19,3},{4,20},{20... | collective-permute-start | bytes 2949128 | tf_op jit(solution)/shard_map/ppermute | solution.py:97
  467.5 43.1 %collective-permute-start.38 = (bf16[192,1280]{1,0:T(8,128)(2,1)}, bf16[192,1280]{1,0:T(8,128)(2,1)}, u32[]{:S(2)}, u32[]{:S(2)}) collective-permute-start(bf16[192,1280]{1,0:T(8,128)(2,1)} %fusion.28), channel_id=1, source_target_pairs={{0,16},{16,0},{1,17},{17,1},{2,18},{18,2},{3,19},{19,3},{4,20},{20... | collective-permute-start | bytes 1474568 | tf_op jit(solution)/shard_map/ppermute | solution.py:97
  469.9 45.9 %collective-permute-start.40 = (bf16[192,1280]{1,0:T(8,128)(2,1)S(1)}, bf16[192,1280]{1,0:T(8,128)(2,1)}, u32[]{:S(2)}, u32[]{:S(2)}) collective-permute-start(bf16[192,1280]{1,0:T(8,128)(2,1)S(1)} %fusion.29), channel_id=1, source_target_pairs={{0,8},{8,0},{1,9},{9,1},{2,10},{10,2},{3,11},{11,3},{4,12},{12,4},... | collective-permute-start | bytes 1474568 | tf_op jit(solution)/shard_map/ppermute | solution.py:97
  471.0 91.5 %all-to-all-start.2 = ((bf16[8,80,512]{2,1,0:T(8,128)(2,1)}), bf16[8,80,512]{2,1,0:T(8,128)(2,1)}, u32[]{:S(2)}, u32[]{:S(2)}) async-start(bf16[8,80,512]{2,1,0:T(8,128)(2,1)} %bitcast.332), calls=%async_computation.4 | async-start | bytes 1310720 | tf_op jit(solution)/shard_map/all_to_all | solution.py:92
  493.8 108.9 %collective-permute-start.66 = (bf16[2,2,320,1280]{3,2,1,0:T(8,128)(2,1)}, bf16[2,2,320,1280]{3,2,1,0:T(8,128)(2,1)}, u32[]{:S(2)}, u32[]{:S(2)}) collective-permute-start(bf16[2,2,320,1280]{3,2,1,0:T(8,128)(2,1)} %dynamic-slice_bitcast_fusion), channel_id=1, source_target_pairs={{0,1},{1,0},{2,3},{3,2},{4,5},{5,4},{6,7},{7,6},{8,9},{9,8},{10,11... | collective-permute-start | bytes 9830408 | tf_op jit(solution)/shard_map/ppermute | solution.py:97
  510.0 99.3 %collective-permute-start.50 = (bf16[2,2,320,1280]{3,2,1,0:T(8,128)(2,1)}, bf16[2,2,320,1280]{3,2,1,0:T(8,128)(2,1)}, u32[]{:S(2)}, u32[]{:S(2)}) collective-permute-start(bf16[2,2,320,1280]{3,2,1,0:T(8,128)(2,1)} %dynamic-slice_bitcast_fusion.1), channel_id=1, source_target_pairs={{0,1},{1,0},{2,3},{3,2},{4,5},{5,4},{6,7},{7,6},{8,9},{9,8},{10,11... | collective-permute-start | bytes 9830408 | tf_op jit(solution)/shard_map/ppermute | solution.py:97
  (99 other events, 1896.7 us)
Sparse Core Ops, SparseCore 0:
  10.1 33.8 all-gather.3
  45.9 113.0 all-gather.5
  206.5 53.4 all-gather.7
  391.9 52.4 reduce-scatter.4
  446.6 105.0 reduce-scatter.2

commit v2 on v1

--- a/solution.py
+++ b/solution.py
@@ -104,98 +104,394 @@
 
 
 def pick(values, index, axis):
-    return lax.dynamic_index_in_dim(values, index, axis, keepdims=False)
+    return lax.dynamic_index_in_dim(values, index, axis, False, allow_negative_indices=False)
+
+
+def behind(here, step, count):
+    return lax.rem(here + (count - step) % count, count)
 
 
 def line_gather(values, axis):
-    count = lax.axis_size(axis)
-    here = lax.axis_index(axis)
     right, left = values, values
     rights, lefts = [], []
-    for _ in range(1, count):
+    for _ in range(1, lax.axis_size(axis)):
         right = slide(right, axis, 1)
         left = slide(left, axis, -1)
         rights.append(right)
         lefts.append(left)
-    pieces = [values]
-    for k in range(1, count):
-        pieces.append(jnp.where(here >= k, rights[k - 1], lefts[count - k - 1]))
-    return pieces
-
-
-def place(pieces, here, dim):
-    count = len(pieces)
-    shape = list(pieces[0].shape)
-    shape.insert(dim, count)
-    buffer = jnp.zeros(shape, pieces[0].dtype)
-    for k, piece in enumerate(pieces):
-        at = [0] * len(shape)
-        at[dim] = (here - k) % count
-        buffer = lax.dynamic_update_slice(buffer, jnp.expand_dims(piece, dim), at)
-    return buffer
-
-
-def reduce_axis(values, axis, dim):
+    return rights, lefts
+
+
+def gather_blocks(pieces, places, rows, count):
+    firsts, pieces = zip(*pieces)
+    columns = pieces[0].shape[1]
+    block = columns
+    while block % (2 * LANES) == 0 and block > 1024:
+        block //= 2
+
+    def kernel(places_ref, *refs):
+        for k, first in enumerate(firsts):
+            refs[-1][places_ref[k], pl.ds(first, pieces[k].shape[0])] = refs[k][...]
+
+    return pl.pallas_call(
+        kernel,
+        grid_spec=pltpu.PrefetchScalarGridSpec(
+            num_scalar_prefetch=1,
+            grid=(columns // block,),
+            in_specs=[
+                pl.BlockSpec((piece.shape[0], block), lambda i, at: (0, i)) for piece in pieces
+            ],
+            out_specs=pl.BlockSpec((count, rows, block), lambda i, at: (0, 0, i)),
+        ),
+        out_shape=jax.ShapeDtypeStruct((count, rows, columns), pieces[0].dtype),
+        cost_estimate=pl.CostEstimate(
+            flops=0, transcendentals=0, bytes_accessed=4 * count * rows * columns
+        ),
+        name="gather_blocks",
+    )(jnp.stack(places).astype(jnp.int32), *pieces)
+
+
+def place_line(z_index, z_count, mine, rights, lefts):
+    group, owned, columns = mine.shape
+    together = 2
+
+    def kernel(z_ref, mine_ref, *refs):
+        out_ref = refs[-1]
+        z = z_ref[0]
+        out_ref[:, z] = mine_ref[...]
+        for k in range(1, z_count):
+
+            @pl.when(z >= k)
+            def _():
+                out_ref[:, z - k] = refs[k - 1][...]
+
+            @pl.when(z + k < z_count)
+            def _():
+                out_ref[:, z + k] = refs[z_count + k - 2][...]
+
+    piece = pl.BlockSpec((together, owned, columns), lambda i, z: (i, 0, 0))
+    placed = pl.pallas_call(
+        kernel,
+        grid_spec=pltpu.PrefetchScalarGridSpec(
+            num_scalar_prefetch=1,
+            grid=(group // together,),
+            in_specs=[piece] * (2 * z_count - 1),
+            out_specs=pl.BlockSpec(
+                (together, z_count, owned, columns), lambda i, z: (i, 0, 0, 0)
+            ),
+        ),
+        out_shape=jax.ShapeDtypeStruct((group, z_count, owned, columns), BF),
+        cost_estimate=pl.CostEstimate(
+            flops=0, transcendentals=0, bytes_accessed=6 * z_count * group * owned * columns
+        ),
+        name="place_line",
+    )(jnp.full((1,), z_index, jnp.int32), mine, *rights, *lefts)
+    return placed.reshape(group * z_count * owned, columns)
+
+
+def split_rows(rows, row_bytes):
+    best = rows
+    for block in range(16, rows, 16):
+        if rows % block == 0 and block * row_bytes > 3 << 20:
+            return block
+    return best
+
+
+def small_kernel(kernel, at, grid, inputs, outputs):
+    moved = sum(array.size * array.dtype.itemsize for array, _, _ in (*inputs, *outputs))
+    return pl.pallas_call(
+        kernel,
+        grid_spec=pltpu.PrefetchScalarGridSpec(
+            num_scalar_prefetch=1,
+            grid=(grid,),
+            in_specs=[pl.BlockSpec(block, index) for _, block, index in inputs],
+            out_specs=[pl.BlockSpec(block, index) for _, block, index in outputs],
+        ),
+        out_shape=[shape for shape, _, _ in outputs],
+        cost_estimate=pl.CostEstimate(flops=0, transcendentals=0, bytes_accessed=moved),
+    )(at, *(array for array, _, _ in inputs))
+
+
+def pair_split(owns, other, at, which):
+    count_a, count_b, rows, columns = other.shape
+    half = rows // 2
+    block = split_rows(half, 12 * count_a * count_b * columns)
+    steps = half // block
+
+    def kernel(at_ref, *refs):
+        a, b = at_ref[0], at_ref[1]
+        mine, (other_0, other_1), outs = refs[: 2 * len(owns)], refs[2 * len(owns) :][:2], refs[2 * len(owns) + 2 :]
+        first = 0
+        for n, own in enumerate(owns):
+            at_columns = pl.ds(first, own.shape[-1])
+            first += own.shape[-1]
+            own_0, own_1 = mine[2 * n : 2 * n + 2]
+            for k in range(count_b):
+                j = lax.rem(b + k, count_b)
+                total = own_0[:, j, 0].astype(F32) + other_0[:, j, :, at_columns].astype(F32)
+                outs[k][:, :, at_columns] = total.astype(BF)
+            for k in range(count_a):
+                i = lax.rem(a + k, count_a)
+                total = own_1[i, :, 0].astype(F32) + other_1[i, :, :, at_columns].astype(F32)
+                outs[count_b + k][:, :, at_columns] = total.astype(BF)
+
+    inputs = [
+        (own, (count_a, count_b, 1, block, own.shape[-1]), index)
+        for own in owns
+        for index in (
+            lambda i, at: (0, 0, at[2] if which else 0, i, 0),
+            lambda i, at: (0, 0, at[2] if which else 0, i + steps, 0),
+        )
+    ]
+    inputs += [
+        (other, (count_a, count_b, block, columns), index)
+        for index in (lambda i, at: (0, 0, i, 0), lambda i, at: (0, 0, i + steps, 0))
+    ]
+    outputs = [
+        (
+            jax.ShapeDtypeStruct((count, half, columns), BF),
+            (count, block, columns),
+            lambda i, at: (0, i, 0),
+        )
+        for count in (count_a,) * count_b + (count_b,) * count_a
+    ]
+    outs = small_kernel(kernel, at, steps, inputs, outputs)
+    return outs[:count_b], outs[count_b:]
+
+
+def sum_split(kept, arrived, at, axes):
+    inputs, outputs = [], []
+    for keep, pieces in zip(kept, arrived):
+        count, half, columns = keep.shape
+        block = split_rows(half, 12 * count * columns)
+        for array in (keep, *pieces):
+            inputs.append((array, (count, block, columns), lambda i, at: (0, i, 0)))
+        for k in range(count):
+            shape = jax.ShapeDtypeStruct((half, columns), BF if k else F32)
+            outputs.append((shape, (block, columns), lambda i, at: (i, 0)))
+    counts = [keep.shape[0] for keep in kept]
+
+    def kernel(at_ref, *refs):
+        ins, outs = list(refs[: len(inputs)]), list(refs[len(inputs) :])
+        for count, pieces, axis in zip(counts, arrived, axes):
+            mine = [ins.pop(0) for _ in range(1 + len(pieces))]
+            for k in range(count):
+                i = lax.rem(at_ref[axis] + k, count)
+                total = mine[0][i].astype(F32)
+                for ref in mine[1:]:
+                    total = total + ref[i].astype(F32)
+                out = outs.pop(0)
+                out[...] = total.astype(out.dtype)
+
+    outs = small_kernel(kernel, at, half // block, inputs, outputs)
+    return (outs[0], outs[1 : counts[0]]), (outs[counts[0]], outs[counts[0] + 1 :])
+
+
+def reduce_plane(owns, other, at, which):
+    other = shift(other, "core", 1)
+    first, second = pair_split(owns, other, at, which)
+    arrived = (
+        [shift(piece, "db", k + 1) for k, piece in enumerate(first[1:])],
+        [shift(piece, "da", k + 1) for k, piece in enumerate(second[1:])],
+    )
+    (kept_0, sends_0), (kept_1, sends_1) = sum_split((first[0], second[0]), arrived, at, (0, 1))
+    arrived_0 = [shift(piece, "da", k + 1) for k, piece in enumerate(sends_0)]
+    arrived_1 = [shift(piece, "db", k + 1) for k, piece in enumerate(sends_1)]
+    return (kept_0, arrived_0), (kept_1, arrived_1)
+
+
+def sum_axis(values, axis, dim):
+    kept, arrived = send_axis(values, axis, dim)
+    for piece in arrived:
+        kept = kept + piece.astype(F32)
+    return kept
+
+
+def send_axis(values, axis, dim):
     count = lax.axis_size(axis)
     here = lax.axis_index(axis)
-    total = pick(values, here, dim).astype(F32)
-    for k in range(1, count):
-        piece = pick(values, (here + k) % count, dim).astype(BF)
-        piece = shift(piece, axis, k)
-        total = total + piece.astype(F32)
-    return total
-
-
-def reduce_plane(values, cut):
-    half = values.shape[cut] // 2
-    first, second = (lax.slice_in_dim(values, i * half, (i + 1) * half, axis=cut) for i in (0, 1))
-    first = reduce_axis(reduce_axis(first, "db", 1), "da", 0)
-    second = reduce_axis(reduce_axis(second, "da", 0), "db", 0)
-    return jnp.concatenate([first, second], cut - 2)
-
-
-def reduce_rows(term, owned_rows, cut):
-    count_a, count_b, count_z = (lax.axis_size(axis) for axis in ("da", "db", "z"))
-    columns = term.shape[1]
-    blocks = term.reshape(count_a, count_b, CORES, count_z * owned_rows, columns)
-    paired = reduce_axis(blocks, "core", 2)
-    plane = reduce_plane(paired.astype(BF), cut)
-    return reduce_axis(plane.reshape(count_z, owned_rows, columns), "z", 0)
-
-
-def reduce_tokens(own, other, rows_here, cut):
-    count_a, count_b = (lax.axis_size(axis) for axis in PAIR)
-    width = own.shape[1]
+    kept = pick(values, here, dim).astype(F32)
+    pieces = [pick(values, behind(here, -k, count), dim).astype(BF) for k in range(1, count)]
+    return kept, [shift(piece, axis, k + 1) for k, piece in enumerate(pieces)]
+
+
+def reduce_plane_fused(own, other):
     other = shift(other, "core", 1)
     paired = (own.astype(F32) + other.astype(F32)).astype(BF)
-    return reduce_plane(paired.reshape(count_a, count_b, rows_here, width), cut)
-
-
-def plane_gather(values):
+    half = own.shape[2] // 2
+    first = sum_axis(paired[:, :, :half], "db", 1)
+    second = sum_axis(paired[:, :, half:], "da", 0)
+    return send_axis(first, "da", 0), send_axis(second, "db", 0)
+
+
+def add_up(refs):
+    total = refs[0][...].astype(F32)
+    for ref in refs[1:]:
+        total = total + ref[...].astype(F32)
+    return total
+
+
+def reduce_tokens(own, other, at):
     count_a, count_b = (lax.axis_size(axis) for axis in PAIR)
-    count = count_a * count_b
+    own, other = (x.reshape(count_a, count_b, -1, x.shape[1]) for x in (own, other))
+    if at is None:
+        return reduce_plane_fused(own, other)
+    return reduce_plane((own[:, :, None],), other, at, 0)
+
+
+def reduce_term(left, right, at):
+    count_a, count_b = (lax.axis_size(axis) for axis in PAIR)
+    term = contract_rows(left, right).astype(BF)
+    term = term.reshape(count_a, count_b, CORES, -1, right.shape[1])
+    core = lax.axis_index("core")
+    other = pick(term, 1 - core, 2)
+    if at is None:
+        return reduce_plane_fused(pick(term, core, 2), other)
+    return reduce_plane((term,), other, at, 2)
+
+
+def reduce_line(terms, at, owned):
+    count_z = lax.axis_size("z")
+    middle = count_z // 2
+    widths = [halves[0][0].shape[-1] for halves in terms]
+    columns = sum(widths)
+    arrays = [
+        array.reshape(middle, owned, -1)
+        for halves in terms
+        for kept, arrived in halves
+        for array in (kept, *arrived)
+    ]
+    splits = [1 + len(arrived) for halves in terms for _, arrived in halves]
+
+    def kernel(at_ref, *refs):
+        ins, outs, all_rows = list(refs[: len(arrays)]), refs[len(arrays) : -1], refs[-1]
+        first = 0
+        for n, size in enumerate(splits):
+            width = widths[n // 2]
+            start = middle * (n % 2)
+            all_rows[start : start + middle, :, first : first + width] = add_up(ins[:size])
+            ins = ins[size:]
+            first += width * (n % 2)
+        for k in range(count_z):
+            outs[k][...] = all_rows[lax.rem(at_ref[3] + k, count_z)].astype(outs[k].dtype)
+
+    kept, *sends = pl.pallas_call(
+        kernel,
+        grid_spec=pltpu.PrefetchScalarGridSpec(
+            num_scalar_prefetch=1,
+            grid=(1,),
+            in_specs=[pl.BlockSpec(array.shape, lambda i, at: (0, 0, 0)) for array in arrays],
+            out_specs=[pl.BlockSpec((owned, columns), lambda i, at: (0, 0))] * count_z,
+            scratch_shapes=[pltpu.VMEM((count_z, owned, columns), F32)],
+        ),
+        out_shape=[
+            jax.ShapeDtypeStruct((owned, columns), BF if k else F32) for k in range(count_z)
+        ],
+        name="row_split",
+    )(at, *arrays)
+    arrived = [shift(piece, "z", k + 1) for k, piece in enumerate(sends)]
+    return [kept, *arrived]
+
+
+def attention_weight_grads(out_terms, qkv_terms, qkv_weight, attn_gain):
+    count = len(out_terms)
+
+    def kernel(*refs):
+        weight_ref, gain_ref, out_ref, qkv_ref, gain_out_ref = refs[2 * count :]
+        out_ref[...] = add_up(refs[:count])
+        grad = add_up(refs[count : 2 * count])
+        qkv_ref[...] = grad
+        gain_sum = jnp.sum(grad * weight_ref[...].astype(F32), 1, keepdims=True)
+        gain_out_ref[...] = gain_sum / gain_ref[...].astype(F32)
+
+    rows = qkv_weight.shape[0]
+    return pl.pallas_call(
+        kernel,
+        out_shape=(
+            jax.ShapeDtypeStruct(out_terms[0].shape, F32),
+            jax.ShapeDtypeStruct(qkv_weight.shape, F32),
+            jax.ShapeDtypeStruct((rows, 1), F32),
+        ),
+        name="attention_weight_grads",
+    )(*out_terms, *qkv_terms, qkv_weight, attn_gain[:, None])
+
+
+def hidden_grads(halves, cot_rows, hidden, inverse, gain):
+    rows, width = cot_rows.shape
+    half = rows // 2
+    block = split_rows(half, 20 * width)
+    steps = half // block
+    terms = [array for kept, arrived in halves for array in (kept, *arrived)]
+    split = 1 + len(halves[0][1])
+    inputs = [
+        (array, (block, width), lambda i, at, n=n: (jnp.clip(i - n * steps, 0, steps - 1), 0))
+        for n, (kept, arrived) in enumerate(halves)
+        for array in (kept, *arrived)
+    ]
+    here = lambda i, at: (i, 0)
+    inputs += [
+        (cot_rows, (block, width), here),
+        (hidden, (block, width), here),
+        (inverse, (block, 1), here),
+        (gain, (1, width), lambda i, at: (0, 0)),
+    ]
+    outputs = [(jax.ShapeDtypeStruct((rows, width), kind), (block, width), here) for kind in (F32, BF)]
+
+    def kernel(at_ref, *refs):
+        cot_ref, hidden_ref, inv_ref, gain_ref, out_ref, low_ref = refs[len(terms) :]
+
+        def finish(parts):
+            value = hidden_ref[...]
+            inv = inv_ref[...]
+            scaled = gain_ref[...] * add_up(parts)
+            mean = jnp.mean(scaled * value, -1, keepdims=True)
+            grad = cot_ref[...].astype(F32) + inv * scaled - value * inv**3 * mean
+            out_ref[...] = grad
+            low_ref[...] = grad.astype(BF)
+
+        @pl.when(pl.program_id(0) < steps)
+        def _():
+            finish(refs[:split])
+
+        @pl.when(pl.program_id(0) >= steps)
+        def _():
+            finish(refs[split : len(terms)])
+
+    return small_kernel(kernel, jnp.zeros((1,), jnp.int32), 2 * steps, inputs, outputs)
+
+
+def plane_gather(values, relay):
+    count_a, count_b = (lax.axis_size(axis) for axis in PAIR)
     here_a, here_b, core = (lax.axis_index(axis) for axis in PLANE)
     rows, width = values.shape
-    buffer = jnp.zeros((count_a, count_b, CORES, rows, width), values.dtype)
-    for ka in range(count_a):
-        for kb in range(count_b):
-            piece = values
-            if ka or kb:
-                pairs = [
-                    (
-                        i,
-                        (i // count_b + ka) % count_a * count_b + (i % count_b + kb) % count_b,
-                    )
-                    for i in range(count)
+    half = rows // 2
+    found = {}
+    for k in range(count_a):
+        found[k, 0] = [(0, shift(values, "da", k))] if k else [(0, values)]
+    for k in range(1, count_b):
+        found[0, k] = [(0, shift(values, "db", k))]
+    for ka in range(1, count_a):
+        for kb in range(1, count_b):
+            if relay:
+                found[ka, kb] = [
+                    (0, shift(found[0, kb][0][1][:half], "da", ka)),
+                    (half, shift(found[ka, 0][0][1][half:], "db", kb)),
                 ]
-                piece = lax.ppermute(values, PAIR, pairs)
+            else:
+                to = [
+                    (i // count_b + ka) % count_a * count_b + (i % count_b + kb) % count_b
+                    for i in range(count_a * count_b)
+                ]
+                found[ka, kb] = [(0, lax.ppermute(values, PAIR, list(enumerate(to))))]
+    pieces, places = [], []
+    for (ka, kb), parts in found.items():
+        chip = behind(here_a, ka, count_a) * count_b + behind(here_b, kb, count_b)
+        for first, piece in parts:
             other = shift(piece, "core", 1)
-            at_a, at_b = (here_a - ka) % count_a, (here_b - kb) % count_b
-            for part, at in ((piece, core), (other, 1 - core)):
-                buffer = lax.dynamic_update_slice(
-                    buffer, part[None, None, None], (at_a, at_b, at, 0, 0)
-                )
-    return buffer.reshape(count * CORES * rows, width)
+            pieces += [(first, piece), (first, other)]
+            places += [chip * CORES + core, chip * CORES + 1 - core]
+    count = count_a * count_b * CORES
+    return gather_blocks(pieces, places, rows, count).reshape(count * rows, width)
 
 
 def hidden_cuts(total, group, part):
@@ -264,10 +560,13 @@
     )(summed)
 
 
-def reorder(values, dp_count, first_count, second_count, addend=None, kind=None):
+def reorder(values, dp_count, first_count, second_count, halves=(), kind=None):
     rows, width = values.shape
     owned = width // (dp_count * first_count * second_count)
     kind = kind or values.dtype
+    half = rows // 2
+    terms = [array for kept, arrived in halves for array in (kept, *arrived)]
+    split = len(terms) // 2
 
     def kernel(*refs):
         out_ref = refs[-1]
@@ -276,15 +575,18 @@
                 for j in range(second_count):
                     source = pl.ds(((d * first_count + i) * second_count + j) * owned, owned)
                     target = pl.ds(((d * second_count + j) * first_count + i) * owned, owned)
-                    piece = refs[0][:, source]
-                    if addend is not None:
-                        piece = piece + refs[1][:, source]
-                    out_ref[:, target] = piece.astype(kind)
-
-    operands = (values,) if addend is None else (values, addend)
+                    if not terms:
+                        out_ref[:, target] = refs[0][:, source].astype(kind)
+                        continue
+                    for n, start in enumerate((0, half)):
+                        piece = refs[0][start : start + half, source]
+                        for ref in refs[1:-1][n * split : (n + 1) * split]:
+                            piece = piece + ref[:, source].astype(F32)
+                        out_ref[start : start + half, target] = piece.astype(kind)
+
     return pl.pallas_call(
         kernel, out_shape=jax.ShapeDtypeStruct((rows, width), kind), name="reorder"
-    )(*operands)
+    )(values, *terms)
 
 
 def attend(rows_in, kv_pieces, cosine, sine_part, query_pos, key_pos):
@@ -468,6 +770,82 @@
     )(core, tokens_in, weight, grad_hidden)
 
 
+def row_product(left, right):
+    tokens, width = left.shape
+    columns = right.shape[1]
+    block = 256 if tokens % 256 == 0 else tokens
+
+    def kernel(left_ref, right_ref, out_ref):
+        out_ref[...] = jnp.dot(left_ref[...], right_ref[...], preferred_element_type=F32)
+
+    return pl.pallas_call(
+        kernel,
+        grid=(tokens // block,),
+        in_specs=[
+            pl.BlockSpec((block, width), lambda i: (i, 0)),
+            pl.BlockSpec((width, columns), lambda i: (0, 0)),
+        ],
+        out_specs=pl.BlockSpec((block, columns), lambda i: (i, 0)),
+        out_shape=jax.ShapeDtypeStruct((tokens, columns), F32),
+        cost_estimate=pl.CostEstimate(
+            flops=2 * tokens * width * columns,
+            transcendentals=0,
+            bytes_accessed=2 * (tokens * width + width * columns) + 4 * tokens * columns,
+        ),
+        name="row_product",
+    )(left, right)
+
+
+def key_value_grads(own, arrived, cosine, sine_part):
+    rows, columns = arrived[0].shape
+
+    def kernel(own_ref, cos_ref, sin_ref, *refs):
+        total = own_ref[...]
+        for ref in refs[:-1]:
+            total = total + ref[...].astype(F32)
+        grad_key = unrotate(total[:, :HEAD], cos_ref[...], sin_ref[...])
+        refs[-1][...] = jnp.concatenate([grad_key, total[:, HEAD:]], 1).astype(BF)
+
+    return pl.pallas_call(
+        kernel, out_shape=jax.ShapeDtypeStruct((rows, columns), BF), name="key_value_grads"
+    )(own, cosine, sine_part, *arrived)
+
+
+def input_grads(grad_query, grad_kv, weight, grad_h, tokens, inverse, gain, counts):
+    rows, width_q = grad_query.shape
+    width = tokens.shape[1]
+    dp_count, z_count = counts
+    owned = width // (dp_count * CORES * z_count)
+
+    def kernel(dq_ref, dkv_ref, weight_ref, grad_ref, token_ref, inv_ref, gain_ref, out_ref, row_ref):
+        last = width_q + grad_kv.shape[1]
+        grad = contract_cols(dq_ref[...], weight_ref[:, :width_q])
+        grad = grad + contract_cols(dkv_ref[...], weight_ref[:, width_q:last])
+        token = token_ref[...].astype(F32)
+        inverse = inv_ref[...]
+        scaled = gain_ref[...] * grad
+        mean = jnp.mean(scaled * token, -1, keepdims=True)
+        row_ref[...] = grad_ref[...] + inverse * scaled - token * inverse**3 * mean
+        for d in range(dp_count):
+            for c in range(CORES):
+                for z in range(z_count):
+                    source = pl.ds(((d * CORES + c) * z_count + z) * owned, owned)
+                    target = pl.ds(((d * z_count + z) * CORES + c) * owned, owned)
+                    out_ref[:, target] = row_ref[:, source]
+
+    return pl.pallas_call(
+        kernel,
+        out_shape=jax.ShapeDtypeStruct((rows, width), F32),
+        scratch_shapes=[pltpu.VMEM((rows, width), F32)],
+        cost_estimate=pl.CostEstimate(
+            flops=2 * rows * width * (width_q + grad_kv.shape[1]),
+            transcendentals=0,
+            bytes_accessed=2 * width * weight.shape[1] + 10 * rows * width,
+        ),
+        name="input_grads",
+    )(grad_query, grad_kv, weight, grad_h, tokens, inverse, gain)
+
+
 def down_product(core, hidden, weight):
     dp_count, _, rows_here, part = hidden.shape
     width = weight.shape[0]
@@ -568,25 +946,22 @@
     packed = pack_shares(ffn_weight, down_weight, group, part)
     mine = exchange(packed, PLANE)
     qkv_line, mine, out_weight = lax.optimization_barrier((qkv_line, mine, out_weight))
-    share = group // 2
-    gate_up_w = jnp.zeros((group, z_count, owned_rows, 2 * part), BF)
-    down_w = jnp.zeros((group, z_count, owned_rows, part), BF)
-    for i in range(2):
-        pieces = line_gather(mine[i * share : (i + 1) * share, None], "z")
-        for k, piece in enumerate(pieces):
-            at = (i * share, (z_index - k) % z_count, 0, 0)
-            gate_up_w = lax.dynamic_update_slice(gate_up_w, piece[..., : 2 * part], at)
-            down_w = lax.dynamic_update_slice(down_w, piece[..., 2 * part :], at)
-    gate_up_w = gate_up_w.reshape(width, 2 * part)
-    down_w = down_w.reshape(width, part)
+    down_mine, gate_up_mine = mine[..., 2 * part :], mine[..., : 2 * part]
+    down_lines = line_gather(down_mine, "z")
+    gate_up_lines = line_gather(gate_up_mine, "z")
+    down_w = place_line(z_index, z_count, down_mine, *down_lines)
+    gate_up_w = place_line(z_index, z_count, gate_up_mine, *gate_up_lines)
     qkv_gain = gather(qkv_line, PLANE)
     qkv_full = qkv_gain[:, :width_qkv]
     gain_one = qkv_gain[:, width_qkv].astype(F32)
     gain_two = qkv_gain[:, width_qkv + 1].astype(F32)
     out_pieces = [out_weight] + [shift(out_weight, "z", k) for k in range(1, z_count)]
-    out_line = place(out_pieces, z_index, 0).reshape(z_count * owned_rows, width_q)
-    out_full = plane_gather(out_line)
-    cot_plane = plane_gather(cot_rows)
+    out_places = [behind(z_index, k, z_count) for k in range(z_count)]
+    out_pieces = [(0, piece) for piece in out_pieces]
+    out_line = gather_blocks(out_pieces, out_places, owned_rows, z_count)
+    out_line = out_line.reshape(z_count * owned_rows, width_q)
+    out_full = plane_gather(out_line, False)
+    cot_plane = plane_gather(cot_rows, True)
 
     positions = (z_index * CORES + core) * rows_here + jnp.arange(rows_here, dtype=jnp.int32)
     cosine, sine_part = rope_tables(positions)
@@ -598,7 +973,7 @@
     kv_rows = jnp.concatenate([keys_own, qkv_rows[:, width_q + HEAD :].astype(jnp.bfloat16)], -1)
     kv_pieces = [kv_rows] + [shift(kv_rows, "z", k) for k in range(1, z_count)]
     kv_pieces = kv_pieces + [shift(piece, "core", 1) for piece in kv_pieces]
-    block_z = (z_index - jnp.arange(z_count, dtype=jnp.int32)) % z_count
+    block_z = lax.rem(z_index + z_count - jnp.arange(z_count, dtype=jnp.int32), z_count)
     block_at = jnp.concatenate([block_z * CORES + core, block_z * CORES + (1 - core)])
     key_pos = (
         block_at[:, None] * rows_here + jnp.arange(rows_here, dtype=jnp.int32)[None, :]
@@ -612,69 +987,58 @@
     normed_two = (hidden_one * inv_two * gain_two).astype(jnp.bfloat16)
 
     normed_plane = gather(normed_two, PLANE)
-    grad_hidden = jnp.dot(cot_plane, down_w, preferred_element_type=jnp.float32)
+    grad_hidden = row_product(cot_plane, down_w)
     core_at = jnp.full((1,), core, jnp.int32)
+    at = jnp.stack([lax.axis_index(axis) for axis in ("da", "db", "core", "z")]).astype(jnp.int32)
     in_blocks = (dp_count, CORES, rows_here, -1)
     hidden, grad_gate_up, dn2_other, dn2_own = feed_forward(
         core_at, normed_plane.reshape(in_blocks), gate_up_w, grad_hidden.reshape(in_blocks)
     )
-    grad_norm_two = reduce_tokens(dn2_own, dn2_other, rows_here, 2)
+    dn2_halves = reduce_tokens(dn2_own, dn2_other, None)
     down_other, down_own = down_product(core_at, hidden, down_w)
-    down_rows = reduce_tokens(down_own, down_other, rows_here, 3)
-    output_rows = reorder(hidden_one, dp_count, CORES, z_count, down_rows, BF)
+    down_halves = reduce_tokens(down_own, down_other, at)
+    output_rows = reorder(hidden_one, dp_count, CORES, z_count, down_halves, BF)
 
     def sum_ffn(left, right):
         right = right.reshape(left.shape[0], -1)
         term = weight_term(left, right, dp_count, z_count).reshape(width, right.shape[1])
-        mine = scatter(term, "z").reshape(group, owned_rows, right.shape[1])
-        return exchange(mine, PLANE)
+        return scatter(term, "z").reshape(group, owned_rows, right.shape[1])
 
     gate_up_sum = sum_ffn(normed_plane, grad_gate_up)
+    gate_up_sum = exchange(gate_up_sum, PLANE)
     down_sum = sum_ffn(cot_plane, hidden)
+    down_sum, gate_up_sum = lax.optimization_barrier((down_sum, gate_up_sum))
+    down_sum = exchange(down_sum, PLANE)
     grad_ffn, gain_two_grad = unpack_gate_up(gate_up_sum, ffn_weight, ffn_gain, group, part)
     gain_two_grad = gain_two_grad[:, 0]
     grad_down = unpack_down(down_sum, FF, group, part)
 
-    scaled_two = gain_two * grad_norm_two
-    grad_h_one = (
-        cot_rows.astype(jnp.float32)
-        + inv_two * scaled_two
-        - hidden_one * inv_two**3 * jnp.mean(scaled_two * hidden_one, -1, keepdims=True)
-    )
-    grad_h_bf = grad_h_one.astype(jnp.bfloat16)
+    grad_h_one, grad_h_bf = hidden_grads(dn2_halves, cot_rows, hidden_one, inv_two, gain_two[None])
     grad_attn = jnp.dot(grad_h_bf, out_full, preferred_element_type=F32).astype(BF)
     grad_query, kv_own, kv_other = attend_back(
         queries, kv_pieces, cosine, sine_part, query_pos, key_pos, log_total, grad_attn
     )
     kv_other = shift(kv_other, "core", 1)
     paired = (kv_own + kv_other.astype(F32)).reshape(z_count, rows_here, 2 * HEAD)
-    own_grad = paired[0]
+    arrived = []
     for k in range(1, z_count):
         piece = paired[k].astype(BF)
-        piece = shift(piece, "z", -k)
-        own_grad = own_grad + piece.astype(F32)
-    grad_key = unrotate(own_grad[:, :HEAD], cosine, sine_part)
-    grad_kv = jnp.concatenate([grad_key, own_grad[:, HEAD:]], -1).astype(BF)
-
-    gout_term = contract_rows(grad_h_bf, attn_flat).astype(BF)
-    gq_term = contract_rows(normed_one, grad_query).astype(BF)
-    gkv_term = contract_rows(normed_one, grad_kv).astype(BF)
-    late_kv = grad_kv + 0.0 * gkv_term[0, 0]
-    grad_norm_one = contract_cols(jnp.concatenate([grad_query, late_kv], -1), qkv_full)
-    scaled_one = gain_one * grad_norm_one
-    grad_rows = (
-        grad_h_one
-        + inv_one * scaled_one
-        - token_f * inv_one**3 * jnp.mean(scaled_one * token_f, -1, keepdims=True)
-    )
-    grad_rows = reorder(grad_rows, dp_count, CORES, z_count)
-
-    grad_out = reduce_rows(gout_term, owned_rows, 3)
-    grad_qkv = jnp.concatenate(
-        [reduce_rows(gq_term, owned_rows, 2), reduce_rows(gkv_term, owned_rows, 2)],
-        1,
-    )
-    gain_one_grad = jnp.sum(grad_qkv * qkv_weight.astype(F32), 1) / attn_gain.astype(F32)
+        arrived.append(shift(piece, "z", -k))
+    grad_kv = key_value_grads(paired[0], arrived, cosine, sine_part)
+
+    grad_rows = input_grads(
+        grad_query, grad_kv, qkv_gain, grad_h_one, tokens, inv_one, gain_one[None], (dp_count, z_count)
+    )
+
+    out_halves = reduce_term(grad_h_bf, attn_flat, at)
+    query_halves = reduce_term(normed_one, grad_query, None)
+    kv_halves = reduce_term(normed_one, grad_kv, None)
+    out_terms = reduce_line([out_halves], at, owned_rows)
+    qkv_terms = reduce_line([query_halves, kv_halves], at, owned_rows)
+    grad_out, grad_qkv, gain_one_grad = attention_weight_grads(
+        out_terms, qkv_terms, qkv_weight, attn_gain
+    )
+    gain_one_grad = gain_one_grad[:, 0]
     return (
         output_rows[None],
         grad_rows[None],

time: 718 us -> 758 us (1.056)
  Pallas kernels: 93.1 us -> 174 us
  other arithmetic: 44.6 us -> 29 us
  local copies, waits for them, and re-layouts: 56.9 us -> 41.3 us
  matrix products: 36.8 us -> 23.5 us
  waiting for transfers between devices: 319 us -> 328 us
    pallas_call x0 -> x16, Pallas kernels: none -> 84.8 us  [the longest x5 25.8 us: small_kernel(): pl.pallas_call(kernel, grid_spec=pltpu.PrefetchScalarGridSpec(num_scalar_...]
    ppermute x56 -> x60, waiting for transfers between devices: 161 us -> 203 us  [shift(): lax.ppermute(values, axis, [(i, (i + step) % count) for i in range(count)])]
    ppermute x6 -> x1, waiting for transfers between devices: 61.9 us -> 32.9 us  [plane_gather(): found[ka, kb] = [(0, lax.ppermute(values, PAIR, list(enumerate(to))))]]
    dynamic_update_slice x36 -> x0, local copies, waits for them, and re-layouts: 27.4 us -> none  [the longest x16 19.6 us: plane_gather(): lax.dynamic_update_slice(buffer, part[None, None, None], (at_a, at_b, at,...]
    all_to_all x2, waiting for transfers between devices: 0.01 us -> 20.1 us  [exchange(): return lax.all_to_all(values, axes, split_axis=0, concat_axis=0, tiled=True)]
    ppermute x12, waiting for transfers between devices: 86.6 us -> 69.9 us  [slide(): return lax.ppermute(values, axis, pairs)]
    broadcast_in_dim x6 -> x0, local copies, waits for them, and re-layouts: 7.83 us -> none  [the longest x2 4.02 us: plane_gather(): buffer = jnp.zeros((count_a, count_b, CORES, rows, width), values.dtype)]
    all_gather x3, waiting for transfers between devices: 9.55 us -> 1.79 us  [gather(): return lax.all_gather(values, axes, axis=axis, tiled=tiled)]
  transfers between devices with their start and end apart: 81 -> 80, of which waited for: 36 -> 32; matrix products, arithmetic and copies ran while one was open for 18% -> 10% of each run, Pallas kernels for 8% -> 19%
where the time goes in v2:
time: 758 us; the launch traced here: 746 us
  waiting for transfers between devices  328 us (43%)
  Pallas kernels  174 us (23%)
  starting transfers between devices  105 us (14%)
  local copies, waits for them, and re-layouts  41.3 us (5%)
  blocking collectives  30.6 us (4%)
  other arithmetic  29 us (4%)
  matrix products  23.5 us (3%)
  between operations  15.2 us (2%)
    ppermute x60, waiting for transfers between devices, shift(): lax.ppermute(values, axis, [(i, (i + step) % count) for i in range(count)])  203 us
    ppermute x12, waiting for transfers between devices, slide(): return lax.ppermute(values, axis, pairs)  69.9 us
    ppermute x60, starting transfers between devices, shift(): lax.ppermute(values, axis, [(i, (i + step) % count) for i in range(count)])  52.4 us
    ppermute x12, starting transfers between devices, slide(): return lax.ppermute(values, axis, pairs)  43.3 us
    ppermute x1, waiting for transfers between devices, plane_gather(): found[ka, kb] = [(0, lax.ppermute(values, PAIR, list(enumerate(to))))]  32.9 us
    all_to_all x1, blocking collectives, exchange(): return lax.all_to_all(values, axes, split_axis=0, concat_axis=0, tiled=True)  30.6 us
    pallas_call x5, Pallas kernels, small_kernel(): pl.pallas_call(kernel, grid_spec=pltpu.PrefetchScalarGridSpec(num_scalar_...  25.8 us
    pallas_call x1, Pallas kernels, feed_forward(): pl.pallas_call(kernel, grid_spec=pltpu.PrefetchScalarGridSpec(num_scalar_...  24.3 us
  transfers between devices with their start and end apart: 80, of which 32 were waited for; matrix products, arithmetic and copies ran while one was open for 10% of the time, Pallas kernels for 19%

profile of v2, /device:TPU:0, one launch (start us, length us, event | category | flops | bytes accessed | tf_op | source)
XLA Modules:
  0.0 746.1 jit_solution(9163212461385031828)
XLA Ops:
  12.6 30.6 %all_to_all.15 = bf16[8,80,1536]{2,1,0:T(8,128)(2,1)} all-to-all(bf16[8,80,1536]{2,1,0:T(8,128)(2,1)} %pack_shares.1), channel_id=1, replica_groups=mesh['da'=2,'db'=2,'z'=4,'core'=2] {'da','db','core'}, dimensions={0} | all-to-all | bytes 3932160 | tf_op jit(solution)/shard_map/all_to_all | solution.py:92
  73.2 24.2 %collective-permute-done.11.refs_2_ = bf16[320,1280]{1,0:T(8,128)(2,1)S(1)} collective-permute-done((bf16[320,1280]{1,0:T(8,128)(2,1)}, bf16[320,1280]{1,0:T(8,128)(2,1)S(1)}, u32[]{:S(2)}, u32[]{:S(2)}) %collective-permute-start.11) | collective-permute-done | bytes 819232 | tf_op jit(solution)/shard_map/ppermute | solution.py:97
  98.4 32.9 %collective-permute-done.15.refs_6_ = bf16[320,1280]{1,0:T(8,128)(2,1)} collective-permute-done((bf16[320,1280]{1,0:T(8,128)(2,1)}, bf16[320,1280]{1,0:T(8,128)(2,1)}, u32[]{:S(2)}, u32[]{:S(2)}) %collective-permute-start.15) | collective-permute-done | bytes 819232 | tf_op jit(solution)/shard_map/ppermute | solution.py:485
  198.0 23.8 %collective-permute-done.26.refs_4_ = bf16[192,2560]{1,0:T(8,128)(2,1)} collective-permute-done((bf16[192,2560]{1,0:T(8,128)(2,1)}, bf16[192,2560]{1,0:T(8,128)(2,1)}, u32[]{:S(2)}, u32[]{:S(2)}) %collective-permute-start.26) | collective-permute-done | bytes 983072 | tf_op jit(solution)/shard_map/ppermute | solution.py:97
  224.7 21.5 %collective-permute-done.28.refs_6_ = bf16[96,2560]{1,0:T(8,128)(2,1)S(1)} collective-permute-done((bf16[96,2560]{1,0:T(8,128)(2,1)S(1)}, bf16[96,2560]{1,0:T(8,128)(2,1)S(1)}, u32[]{:S(2)}, u32[]{:S(2)}) %collective-permute-start.28) | collective-permute-done | bytes 491552 | tf_op jit(solution)/shard_map/ppermute | solution.py:97
  246.7 8.8 %collective-permute-start.18 = (bf16[8,80,1024]{2,1,0:T(8,128)(2,1)S(1)}, bf16[8,80,1024]{2,1,0:T(8,128)(2,1)}, u32[]{:S(2)}, u32[]{:S(2)}) collective-permute-start(bf16[8,80,1024]{2,1,0:T(8,128)(2,1)S(1)} %collective-permute-done.17.refs_0_), channel_id=1, source_target_pairs={{0,2},{2,4},{4,6},{1,3},{3,5},{5,7},{8,10},{10,12},{12,14},{9,11},... | collective-permute-start | bytes 3932168 | tf_op jit(solution)/shard_map/ppermute | solution.py:103
  264.0 33.2 %collective-permute-done.32.refs_0_ = bf16[8,80,512]{2,1,0:T(8,128)(2,1)S(1)} collective-permute-done((bf16[8,80,512]{2,1,0:T(8,128)(2,1)S(1)}, bf16[8,80,512]{2,1,0:T(8,128)(2,1)S(1)}, u32[]{:S(2)}, u32[]{:S(2)}) %collective-permute-start.32) | collective-permute-done | bytes 655392 | tf_op jit(solution)/shard_map/ppermute | solution.py:103
  324.0 7.6 %gather_blocks.5 = bf16[8,192,2560]{2,1,0:T(8,128)(2,1)} custom-call(s32[10]{0:T(128)} %stack.101.places_ref, bf16[192,2560]{1,0:T(8,128)(2,1)} %reorder.4.refs_0_.refs_4_, bf16[192,2560]{1,0:T(8,128)(2,1)} %copy-done.22, bf16[192,2560]{1,0:T(8,128)(2,1)} %copy-done.16, bf16[192,2560]{1,0:T(8,128)(2,1)} %copy-done.23, ...), custom_call_target="tpu_custom_call" | custom-call | bytes 15728640 | tf_op jit(solution)/shard_map/gather_blocks/pallas_call | solution.py:136
  331.6 26.0 %collective-permute-done.34.refs_2_ = bf16[8,80,512]{2,1,0:T(8,128)(2,1)} collective-permute-done((bf16[8,80,512]{2,1,0:T(8,128)(2,1)}, bf16[8,80,512]{2,1,0:T(8,128)(2,1)}, u32[]{:S(2)}, u32[]{:S(2)}) %collective-permute-start.34) | collective-permute-done | bytes 655392 | tf_op jit(solution)/shard_map/ppermute | solution.py:103
  367.0 9.5 %row_product.1 = f32[1536,512]{1,0:T(8,128)} custom-call(bf16[1536,2560]{1,0:T(8,128)(2,1)} %bitcast.136, bf16[2560,512]{1,0:T(8,128)(2,1)} %bitcast.148), custom_call_target="tpu_custom_call" | custom-call | flops 4026531840 | bytes 13631488 | tf_op jit(solution)/shard_map/row_product/pallas_call | solution.py:781
  382.7 24.3 %feed_forward.1 = (bf16[4,2,192,512]{3,2,1,0:T(8,128)(2,1)}, bf16[4,2,192,1024]{3,2,1,0:T(8,128)(2,1)}, bf16[768,2560]{1,0:T(8,128)(2,1)}, bf16[768,2560]{1,0:T(8,128)(2,1)}) custom-call(s32[1]{0:T(128)} %bitcast.19.core_ref, bf16[4,2,192,2560]{3,2,1,0:T(8,128)(2,1)} %bitcast.171, bf16[2560,1024]{1,0:T(8,128)(2,1)} %bitcast.139, f32[4,2,192,512]{3,2,1,0:T(8,128)} %bitcast.174), custom_call_target="tpu_custom_call" | custom-call | flops 16106127360 | bytes 28835840 | tf_op jit(solution)/shard_map/feed_forward/pallas_call | solution.py:746
  407.0 12.5 %weight_term.3 = bf16[4,4,2,80,1024]{4,3,2,1,0:T(8,128)(2,1)} custom-call(bf16[1536,2560]{1,0:T(8,128)(2,1)} %all-gather.8.cloned.1.call-done.left_ref, bf16[1536,1024]{1,0:T(8,128)(2,1)} %bitcast.175), custom_call_target="tpu_custom_call" | custom-call | flops 8053063680 | bytes 16252928 | tf_op jit(solution)/shard_map/weight_term/pallas_call | solution.py:904
  429.4 9.6 %down_product.1 = (bf16[768,2560]{1,0:T(8,128)(2,1)}, bf16[768,2560]{1,0:T(8,128)(2,1)}) custom-call(s32[1]{0:T(128)} %bitcast.19.core_ref, bf16[4,2,192,512]{3,2,1,0:T(8,128)(2,1)} %get-tuple-element.60.in_ref, bf16[2560,512]{1,0:T(8,128)(2,1)} %bitcast.149), custom_call_target="tpu_custom_call" | custom-call | flops 4026531840 | bytes 12058624 | tf_op jit(solution)/shard_map/down_product/pallas_call | solution.py:868
  440.9 10.1 %collective-permute-done.46 = bf16[2,96,2560]{2,1,0:T(8,128)(2,1)} collective-permute-done((bf16[2,96,2560]{2,1,0:T(8,128)(2,1)}, bf16[2,96,2560]{2,1,0:T(8,128)(2,1)}, u32[]{:S(2)}, u32[]{:S(2)}) %collective-permute-start.46) | collective-permute-done | bytes 983072 | tf_op jit(solution)/shard_map/ppermute | solution.py:97
  453.9 10.0 %collective-permute-done.44 = bf16[2,96,2560]{2,1,0:T(8,128)(2,1)S(1)} collective-permute-done((bf16[2,96,2560]{2,1,0:T(8,128)(2,1)S(1)}, bf16[2,96,2560]{2,1,0:T(8,128)(2,1)S(1)}, u32[]{:S(2)}, u32[]{:S(2)}) %collective-permute-start.44) | collective-permute-done | bytes 983072 | tf_op jit(solution)/shard_map/ppermute | solution.py:97
  487.2 8.8 %attend_back.1 = (bf16[192,1280]{1,0:T(8,128)(2,1)}, f32[768,512]{1,0:T(8,128)}, bf16[768,512]{1,0:T(8,128)(2,1)}) custom-call(bf16[192,512]{1,0:T(8,128)(2,1)} %pad_maximum_fusion.refs_0_, bf16[192,512]{1,0:T(8,128)(2,1)} %collective-permute-done.refs_1_, bf16[192,512]{1,0:T(8,128)(2,1)} %copy-done.54, bf16[192,512]{1,0:T(8,128)(2,1)} %copy-done.55, ...), custom_call_target="tpu_custom_call" | custom-call | flops 3774873600 | bytes 5210112 | tf_op jit(solution)/shard_map/attend_back/pallas_call | solution.py:677
  504.3 8.6 %collective-permute-done.49.refs_0_ = bf16[192,512]{1,0:T(8,128)(2,1)S(1)} collective-permute-done((bf16[192,512]{1,0:T(8,128)(2,1)S(1)}, bf16[192,512]{1,0:T(8,128)(2,1)S(1)}, u32[]{:S(2)}, u32[]{:S(2)}) %collective-permute-start.49) | collective-permute-done | bytes 196640 | tf_op jit(solution)/shard_map/ppermute | solution.py:97
  512.9 15.2 %collective-permute-done.50.refs_1_ = bf16[192,512]{1,0:T(8,128)(2,1)S(1)} collective-permute-done((bf16[192,512]{1,0:T(8,128)(2,1)S(1)}, bf16[192,512]{1,0:T(8,128)(2,1)S(1)}, u32[]{:S(2)}, u32[]{:S(2)}) %collective-permute-start.50) | collective-permute-done | bytes 196640 | tf_op jit(solution)/shard_map/ppermute | solution.py:97
  552.6 8.5 %weight_term.2 = bf16[4,4,2,80,512]{4,3,2,1,0:T(8,128)(2,1)} custom-call(bf16[1536,2560]{1,0:T(8,128)(2,1)} %bitcast.137, bf16[1536,512]{1,0:T(8,128)(2,1)} %bitcast.176), custom_call_target="tpu_custom_call" | custom-call | flops 4026531840 | bytes 12058624 | tf_op jit(solution)/shard_map/weight_term/pallas_call | solution.py:904
  597.8 13.9 %collective-permute-done.53.refs_1_ = bf16[2,160,1280]{2,1,0:T(8,128)(2,1)} collective-permute-done((bf16[2,160,1280]{2,1,0:T(8,128)(2,1)}, bf16[2,160,1280]{2,1,0:T(8,128)(2,1)}, u32[]{:S(2)}, u32[]{:S(2)}) %collective-permute-start.53) | collective-permute-done | bytes 819232 | tf_op jit(solution)/shard_map/ppermute | solution.py:97
  612.9 9.4 %collective-permute-done.54.refs_3_ = bf16[2,160,1280]{2,1,0:T(8,128)(2,1)} collective-permute-done((bf16[2,160,1280]{2,1,0:T(8,128)(2,1)}, bf16[2,160,1280]{2,1,0:T(8,128)(2,1)}, u32[]{:S(2)}, u32[]{:S(2)}) %collective-permute-start.54) | collective-permute-done | bytes 819232 | tf_op jit(solution)/shard_map/ppermute | solution.py:97
  638.0 20.1 %all-to-all-done.1.sum_ref = bf16[8,80,1024]{2,1,0:T(8,128)(2,1)} async-done(((bf16[8,80,1024]{2,1,0:T(8,128)(2,1)}), bf16[8,80,1024]{2,1,0:T(8,128)(2,1)}, u32[]{:S(2)}, u32[]{:S(2)}) %all-to-all-start.1) | async-done | bytes 1310752 | tf_op jit(solution)/shard_map/all_to_all | solution.py:92
  702.1 10.6 %input_grads.1 = f32[192,2560]{1,0:T(8,128)} custom-call(bf16[192,1280]{1,0:T(8,128)(2,1)} %get-tuple-element.76.dq_ref, bf16[192,512]{1,0:T(8,128)(2,1)} %key_value_grads.1.dkv_ref, bf16[2560,1920]{1,0:T(8,128)(2,1)} %all-gather.6.cloned.1.call-done.weight_ref, f32[192,2560]{1,0:T(8,128)} %get-tuple-element.79.grad_ref, ...), custom_call_target="tpu_custom_call" | custom-call | flops 1761607680 | bytes 14745600 | tf_op jit(solution)/shard_map/input_grads/pallas_call | solution.py:836
  712.8 13.1 %collective-permute-done.58.refs_2_ = bf16[80,1280]{1,0:T(8,128)(2,1)S(1)} collective-permute-done((bf16[80,1280]{1,0:T(8,128)(2,1)S(1)}, bf16[80,1280]{1,0:T(8,128)(2,1)S(1)}, u32[]{:S(2)}, u32[]{:S(2)}) %collective-permute-start.58) | collective-permute-done | bytes 204832 | tf_op jit(solution)/shard_map/ppermute | solution.py:97
  (366 shorter events, 338.4 us)
Async XLA Ops:
  9.7 122.7 %all-gather.6.cloned.1.call-start = ((), (), s32[]{:S(2)}) async-start(), calls=%async_computation.6 | async-start | bytes 11059200 | tf_op jit(solution)/shard_map/all_gather | solution.py:84
  44.0 338.7 %all-gather.8.cloned.1.call-start = ((), (), s32[]{:S(2)}) async-start(), calls=%async_computation.7 | async-start | bytes 8847360 | tf_op jit(solution)/shard_map/all_gather | solution.py:84
  68.0 63.4 %collective-permute-start.15 = (bf16[320,1280]{1,0:T(8,128)(2,1)}, bf16[320,1280]{1,0:T(8,128)(2,1)}, u32[]{:S(2)}, u32[]{:S(2)}) collective-permute-start(bf16[320,1280]{1,0:T(8,128)(2,1)} %bitcast.143), channel_id=1, source_target_pairs={{0,24},{8,16},{16,8},{24,0},{1,25},{9,17},{17,9},{25,1},{2,26},{10... | collective-permute-start | bytes 2457608 | tf_op jit(solution)/shard_map/ppermute | solution.py:485
  73.1 71.7 %collective-permute-start.10 = (bf16[320,1280]{1,0:T(8,128)(2,1)S(1)}, bf16[320,1280]{1,0:T(8,128)(2,1)}, u32[]{:S(2)}, u32[]{:S(2)}) collective-permute-start(bf16[320,1280]{1,0:T(8,128)(2,1)S(1)} %bitcast.145), channel_id=1, source_target_pairs={{0,1},{1,0},{2,3},{3,2},{4,5},{5,4},{6,7},{7,6},{8,9},{9,8},{10,11... | collective-permute-start | bytes 2457608 | tf_op jit(solution)/shard_map/ppermute | solution.py:97
  97.4 48.3 %collective-permute-start.12 = (bf16[320,1280]{1,0:T(8,128)(2,1)S(1)}, bf16[320,1280]{1,0:T(8,128)(2,1)}, u32[]{:S(2)}, u32[]{:S(2)}) collective-permute-start(bf16[320,1280]{1,0:T(8,128)(2,1)S(1)} %collective-permute-done.11.refs_2_), channel_id=1, source_target_pairs={{0,1},{1,0},{2,3},{3,2},{4,5},{5,4},{6,7},{7,6},{8,9},{9,8},{10,11... | collective-permute-start | bytes 2457608 | tf_op jit(solution)/shard_map/ppermute | solution.py:97
  98.4 48.8 %collective-permute-start.14 = (bf16[320,1280]{1,0:T(8,128)(2,1)S(1)}, bf16[320,1280]{1,0:T(8,128)(2,1)}, u32[]{:S(2)}, u32[]{:S(2)}) collective-permute-start(bf16[320,1280]{1,0:T(8,128)(2,1)S(1)} %collective-permute-done.13.refs_4_), channel_id=1, source_target_pairs={{0,1},{1,0},{2,3},{3,2},{4,5},{5,4},{6,7},{7,6},{8,9},{9,8},{10,11... | collective-permute-start | bytes 2457608 | tf_op jit(solution)/shard_map/ppermute | solution.py:97
  183.0 444.0 %reduce-scatter.5.cloned.1.call-start = ((), (), s32[]{:S(2)}) async-start(), calls=%async_computation.9 | async-start | bytes 6553600 | tf_op jit(solution)/shard_map/reduce_scatter | solution.py:88
  190.4 56.3 %collective-permute-start.17 = (bf16[8,80,1024]{2,1,0:T(8,128)(2,1)S(1)}, bf16[8,80,1024]{2,1,0:T(8,128)(2,1)S(1)}, u32[]{:S(2)}, u32[]{:S(2)}) collective-permute-start(bf16[8,80,1024]{2,1,0:T(8,128)(2,1)S(1)} %slice.77.mine_ref), channel_id=1, source_target_pairs={{0,2},{2,4},{4,6},{1,3},{3,5},{5,7},{8,10},{10,12},{12,14},{9,11},... | collective-permute-start | bytes 3932168 | tf_op jit(solution)/shard_map/ppermute | solution.py:103
  196.6 58.9 %collective-permute-start.20 = (bf16[8,80,1024]{2,1,0:T(8,128)(2,1)S(1)}, bf16[8,80,1024]{2,1,0:T(8,128)(2,1)S(1)}, u32[]{:S(2)}, u32[]{:S(2)}) collective-permute-start(bf16[8,80,1024]{2,1,0:T(8,128)(2,1)S(1)} %slice.77.mine_ref), channel_id=1, source_target_pairs={{2,0},{4,2},{6,4},{3,1},{5,3},{7,5},{10,8},{12,10},{14,12},{11,9},... | collective-permute-start | bytes 3932168 | tf_op jit(solution)/shard_map/ppermute | solution.py:103
  197.9 60.0 %collective-permute-start.23 = (bf16[192,2560]{1,0:T(8,128)(2,1)S(1)}, bf16[192,2560]{1,0:T(8,128)(2,1)S(1)}, u32[]{:S(2)}, u32[]{:S(2)}) collective-permute-start(bf16[192,2560]{1,0:T(8,128)(2,1)S(1)} %copy-done.4), channel_id=1, source_target_pairs={{0,1},{1,0},{2,3},{3,2},{4,5},{5,4},{6,7},{7,6},{8,9},{9,8},{10,11... | collective-permute-start | bytes 2949128 | tf_op jit(solution)/shard_map/ppermute | solution.py:97
  246.7 57.1 %collective-permute-start.18 = (bf16[8,80,1024]{2,1,0:T(8,128)(2,1)S(1)}, bf16[8,80,1024]{2,1,0:T(8,128)(2,1)}, u32[]{:S(2)}, u32[]{:S(2)}) collective-permute-start(bf16[8,80,1024]{2,1,0:T(8,128)(2,1)S(1)} %collective-permute-done.17.refs_0_), channel_id=1, source_target_pairs={{0,2},{2,4},{4,6},{1,3},{3,5},{5,7},{8,10},{10,12},{12,14},{9,11},... | collective-permute-start | bytes 3932168 | tf_op jit(solution)/shard_map/ppermute | solution.py:103
  255.5 54.0 %collective-permute-start.21 = (bf16[8,80,1024]{2,1,0:T(8,128)(2,1)S(1)}, bf16[8,80,1024]{2,1,0:T(8,128)(2,1)}, u32[]{:S(2)}, u32[]{:S(2)}) collective-permute-start(bf16[8,80,1024]{2,1,0:T(8,128)(2,1)S(1)} %collective-permute-done.20.refs_3_), channel_id=1, source_target_pairs={{2,0},{4,2},{6,4},{3,1},{5,3},{7,5},{10,8},{12,10},{14,12},{11,9},... | collective-permute-start | bytes 3932168 | tf_op jit(solution)/shard_map/ppermute | solution.py:103
  258.0 45.7 %collective-permute-start.25 = (bf16[192,2560]{1,0:T(8,128)(2,1)S(1)}, bf16[192,2560]{1,0:T(8,128)(2,1)S(1)}, u32[]{:S(2)}, u32[]{:S(2)}) collective-permute-start(bf16[192,2560]{1,0:T(8,128)(2,1)S(1)} %collective-permute-done.24.refs_2_), channel_id=1, source_target_pairs={{0,1},{1,0},{2,3},{3,2},{4,5},{5,4},{6,7},{7,6},{8,9},{9,8},{10,11... | collective-permute-start | bytes 2949128 | tf_op jit(solution)/shard_map/ppermute | solution.py:97
  303.8 72.7 %collective-permute-start.19 = (bf16[8,80,1024]{2,1,0:T(8,128)(2,1)}, bf16[8,80,1024]{2,1,0:T(8,128)(2,1)}, u32[]{:S(2)}, u32[]{:S(2)}) collective-permute-start(bf16[8,80,1024]{2,1,0:T(8,128)(2,1)} %collective-permute-done.18.refs_1_), channel_id=1, source_target_pairs={{0,2},{2,4},{4,6},{1,3},{3,5},{5,7},{8,10},{10,12},{12,14},{9,11},... | collective-permute-start | bytes 3932168 | tf_op jit(solution)/shard_map/ppermute | solution.py:103
  309.5 67.0 %collective-permute-start.22 = (bf16[8,80,1024]{2,1,0:T(8,128)(2,1)}, bf16[8,80,1024]{2,1,0:T(8,128)(2,1)}, u32[]{:S(2)}, u32[]{:S(2)}) collective-permute-start(bf16[8,80,1024]{2,1,0:T(8,128)(2,1)} %collective-permute-done.21.refs_4_), channel_id=1, source_target_pairs={{2,0},{4,2},{6,4},{3,1},{5,3},{7,5},{10,8},{12,10},{14,12},{11,9},... | collective-permute-start | bytes 3932168 | tf_op jit(solution)/shard_map/ppermute | solution.py:103
  316.6 40.9 %collective-permute-start.34 = (bf16[8,80,512]{2,1,0:T(8,128)(2,1)}, bf16[8,80,512]{2,1,0:T(8,128)(2,1)}, u32[]{:S(2)}, u32[]{:S(2)}) collective-permute-start(bf16[8,80,512]{2,1,0:T(8,128)(2,1)} %collective-permute-done.33.refs_1_), channel_id=1, source_target_pairs={{0,2},{2,4},{4,6},{1,3},{3,5},{5,7},{8,10},{10,12},{12,14},{9,11},... | collective-permute-start | bytes 1966088 | tf_op jit(solution)/shard_map/ppermute | solution.py:103
  322.0 40.5 %collective-permute-start.37 = (bf16[8,80,512]{2,1,0:T(8,128)(2,1)}, bf16[8,80,512]{2,1,0:T(8,128)(2,1)}, u32[]{:S(2)}, u32[]{:S(2)}) collective-permute-start(bf16[8,80,512]{2,1,0:T(8,128)(2,1)} %collective-permute-done.36.refs_4_), channel_id=1, source_target_pairs={{2,0},{4,2},{6,4},{3,1},{5,3},{7,5},{10,8},{12,10},{14,12},{11,9},... | collective-permute-start | bytes 1966088 | tf_op jit(solution)/shard_map/ppermute | solution.py:103
  419.5 218.5 %reduce-scatter.3.cloned.1.call-start = ((), (), s32[]{:S(2)}) async-start(), calls=%async_computation.8 | async-start | bytes 3276800 | tf_op jit(solution)/shard_map/reduce_scatter | solution.py:88
  438.9 97.9 %collective-permute-start.38 = (bf16[2,2,192,2560]{3,2,1,0:T(8,128)(2,1)}, bf16[2,2,192,2560]{3,2,1,0:T(8,128)(2,1)}, u32[]{:S(2)}, u32[]{:S(2)}) collective-permute-start(bf16[2,2,192,2560]{3,2,1,0:T(8,128)(2,1)} %bitcast.172), channel_id=1, source_target_pairs={{0,1},{1,0},{2,3},{3,2},{4,5},{5,4},{6,7},{7,6},{8,9},{9,8},{10,11... | collective-permute-start | bytes 11796488 | tf_op jit(solution)/shard_map/ppermute | solution.py:97
  503.5 74.5 %collective-permute-start.60 = (bf16[2,2,320,1280]{3,2,1,0:T(8,128)(2,1)}, bf16[2,2,320,1280]{3,2,1,0:T(8,128)(2,1)}, u32[]{:S(2)}, u32[]{:S(2)}) collective-permute-start(bf16[2,2,320,1280]{3,2,1,0:T(8,128)(2,1)} %dynamic-slice_bitcast_fusion), channel_id=1, source_target_pairs={{0,1},{1,0},{2,3},{3,2},{4,5},{5,4},{6,7},{7,6},{8,9},{9,8},{10,11... | collective-permute-start | bytes 9830408 | tf_op jit(solution)/shard_map/ppermute | solution.py:97
  575.0 113.2 %collective-permute-start.41 = (bf16[96,2560]{1,0:T(8,128)(2,1)}, bf16[96,2560]{1,0:T(8,128)(2,1)}, u32[]{:S(2)}, u32[]{:S(2)}) collective-permute-start(bf16[96,2560]{1,0:T(8,128)(2,1)} %get-tuple-element.68), channel_id=1, source_target_pairs={{0,16},{16,0},{1,17},{17,1},{2,18},{18,2},{3,19},{19,3},{4,20},{20... | collective-permute-start | bytes 1474568 | tf_op jit(solution)/shard_map/ppermute | solution.py:97
  584.4 47.0 %collective-permute-start.63 = (bf16[2,160,1280]{2,1,0:T(8,128)(2,1)}, bf16[2,160,1280]{2,1,0:T(8,128)(2,1)}, u32[]{:S(2)}, u32[]{:S(2)}) collective-permute-start(bf16[2,160,1280]{2,1,0:T(8,128)(2,1)} %dynamic-slice_bitcast_fusion.7), channel_id=1, source_target_pairs={{0,16},{16,0},{1,17},{17,1},{2,18},{18,2},{3,19},{19,3},{4,20},{20... | collective-permute-start | bytes 2457608 | tf_op jit(solution)/shard_map/ppermute | solution.py:97
  611.7 80.3 %collective-permute-start.42 = (bf16[96,2560]{1,0:T(8,128)(2,1)}, bf16[96,2560]{1,0:T(8,128)(2,1)S(1)}, u32[]{:S(2)}, u32[]{:S(2)}) collective-permute-start(bf16[96,2560]{1,0:T(8,128)(2,1)} %get-tuple-element.70), channel_id=1, source_target_pairs={{0,8},{8,0},{1,9},{9,1},{2,10},{10,2},{3,11},{11,3},{4,12},{12,4},... | collective-permute-start | bytes 1474568 | tf_op jit(solution)/shard_map/ppermute | solution.py:97
  658.1 77.9 %all-to-all-start.2 = ((bf16[8,80,512]{2,1,0:T(8,128)(2,1)}), bf16[8,80,512]{2,1,0:T(8,128)(2,1)S(1)}, u32[]{:S(2)}, u32[]{:S(2)}) async-start(bf16[8,80,512]{2,1,0:T(8,128)(2,1)} %bitcast.162), calls=%async_computation.4 | async-start | bytes 1310720 | tf_op jit(solution)/shard_map/all_to_all | solution.py:92
  (116 other events, 2446.3 us)
Sparse Core Ops, SparseCore 0:
  10.1 33.8 all-gather.3
  45.9 86.4 all-gather.5
  182.9 75.5 all-gather.7
  419.7 98.6 reduce-scatter.4
  561.2 48.7 reduce-scatter.2

commit v3 on v2

--- a/solution.py
+++ b/solution.py
@@ -393,27 +393,29 @@
     return [kept, *arrived]
 
 
-def attention_weight_grads(out_terms, qkv_terms, qkv_weight, attn_gain):
-    count = len(out_terms)
+def attention_weight_grads(terms, qkv_weight, attn_gain):
+    rows, width_qkv = qkv_weight.shape
+    width_out = terms[0].shape[1] - width_qkv
+    count = len(terms)
 
     def kernel(*refs):
-        weight_ref, gain_ref, out_ref, qkv_ref, gain_out_ref = refs[2 * count :]
-        out_ref[...] = add_up(refs[:count])
-        grad = add_up(refs[count : 2 * count])
+        weight_ref, gain_ref, out_ref, qkv_ref, gain_out_ref = refs[count:]
+        total = add_up(refs[:count])
+        out_ref[...] = total[:, :width_out]
+        grad = total[:, width_out:]
         qkv_ref[...] = grad
         gain_sum = jnp.sum(grad * weight_ref[...].astype(F32), 1, keepdims=True)
         gain_out_ref[...] = gain_sum / gain_ref[...].astype(F32)
 
-    rows = qkv_weight.shape[0]
     return pl.pallas_call(
         kernel,
         out_shape=(
-            jax.ShapeDtypeStruct(out_terms[0].shape, F32),
-            jax.ShapeDtypeStruct(qkv_weight.shape, F32),
+            jax.ShapeDtypeStruct((rows, width_out), F32),
+            jax.ShapeDtypeStruct((rows, width_qkv), F32),
             jax.ShapeDtypeStruct((rows, 1), F32),
         ),
         name="attention_weight_grads",
-    )(*out_terms, *qkv_terms, qkv_weight, attn_gain[:, None])
+    )(*terms, qkv_weight, attn_gain[:, None])
 
 
 def hidden_grads(halves, cot_rows, hidden, inverse, gain):
@@ -1033,11 +1035,8 @@
     out_halves = reduce_term(grad_h_bf, attn_flat, at)
     query_halves = reduce_term(normed_one, grad_query, None)
     kv_halves = reduce_term(normed_one, grad_kv, None)
-    out_terms = reduce_line([out_halves], at, owned_rows)
-    qkv_terms = reduce_line([query_halves, kv_halves], at, owned_rows)
-    grad_out, grad_qkv, gain_one_grad = attention_weight_grads(
-        out_terms, qkv_terms, qkv_weight, attn_gain
-    )
+    terms = reduce_line([out_halves, query_halves, kv_halves], at, owned_rows)
+    grad_out, grad_qkv, gain_one_grad = attention_weight_grads(terms, qkv_weight, attn_gain)
     gain_one_grad = gain_one_grad[:, 0]
     return (
         output_rows[None],

time: 758 us -> 744 us (0.982)
  the two profiles are of different devices: /device:TPU:0 before, /device:TPU:8 now
where the time goes in v3:
time: 744 us; the launch traced here: 734 us
  waiting for transfers between devices  328 us (44%)
  Pallas kernels  172 us (23%)
  starting transfers between devices  96.1 us (13%)
  local copies, waits for them, and re-layouts  41.9 us (6%)
  blocking collectives  29.6 us (4%)
  other arithmetic  27.7 us (4%)
  matrix products  23.5 us (3%)
  between operations  15.2 us (2%)
    ppermute x57, waiting for transfers between devices, shift(): lax.ppermute(values, axis, [(i, (i + step) % count) for i in range(count)])  226 us
    ppermute x12, waiting for transfers between devices, slide(): return lax.ppermute(values, axis, pairs)  66.8 us
    ppermute x57, starting transfers between devices, shift(): lax.ppermute(values, axis, [(i, (i + step) % count) for i in range(count)])  48.1 us
    ppermute x12, starting transfers between devices, slide(): return lax.ppermute(values, axis, pairs)  39 us
    ppermute x1, waiting for transfers between devices, plane_gather(): found[ka, kb] = [(0, lax.ppermute(values, PAIR, list(enumerate(to))))]  29.9 us
    all_to_all x1, blocking collectives, exchange(): return lax.all_to_all(values, axes, split_axis=0, concat_axis=0, tiled=True)  29.6 us
    pallas_call x5, Pallas kernels, small_kernel(): pl.pallas_call(kernel, grid_spec=pltpu.PrefetchScalarGridSpec(num_scalar_...  25.6 us
    pallas_call x1, Pallas kernels, feed_forward(): pl.pallas_call(kernel, grid_spec=pltpu.PrefetchScalarGridSpec(num_scalar_...  24.3 us
  transfers between devices with their start and end apart: 77, of which 37 were waited for; matrix products, arithmetic and copies ran while one was open for 10% of the time, Pallas kernels for 19%

profile of v3, /device:TPU:8, one launch (start us, length us, event | category | flops | bytes accessed | tf_op | source)
XLA Modules:
  0.0 733.9 jit_solution(4920905443798147954)
XLA Ops:
  12.6 29.6 %all_to_all.15 = bf16[8,80,1536]{2,1,0:T(8,128)(2,1)} all-to-all(bf16[8,80,1536]{2,1,0:T(8,128)(2,1)} %pack_shares.1), channel_id=1, replica_groups=mesh['da'=2,'db'=2,'z'=4,'core'=2] {'da','db','core'}, dimensions={0} | all-to-all | bytes 3932160 | tf_op jit(solution)/shard_map/all_to_all | solution.py:92
  47.6 10.6 %collective-permute-done.7.refs_1_ = bf16[80,1280]{1,0:T(8,128)(2,1)S(1)} collective-permute-done((bf16[80,1280]{1,0:T(8,128)(2,1)S(1)}, bf16[80,1280]{1,0:T(8,128)(2,1)S(1)}, u32[]{:S(2)}, u32[]{:S(2)}) %collective-permute-start.7) | collective-permute-done | bytes 204832 | tf_op jit(solution)/shard_map/ppermute | solution.py:97
  74.3 24.7 %collective-permute-done.11.refs_2_ = bf16[320,1280]{1,0:T(8,128)(2,1)S(1)} collective-permute-done((bf16[320,1280]{1,0:T(8,128)(2,1)}, bf16[320,1280]{1,0:T(8,128)(2,1)S(1)}, u32[]{:S(2)}, u32[]{:S(2)}) %collective-permute-start.11) | collective-permute-done | bytes 819232 | tf_op jit(solution)/shard_map/ppermute | solution.py:97
  102.0 29.9 %collective-permute-done.15.refs_6_ = bf16[320,1280]{1,0:T(8,128)(2,1)} collective-permute-done((bf16[320,1280]{1,0:T(8,128)(2,1)}, bf16[320,1280]{1,0:T(8,128)(2,1)}, u32[]{:S(2)}, u32[]{:S(2)}) %collective-permute-start.15) | collective-permute-done | bytes 819232 | tf_op jit(solution)/shard_map/ppermute | solution.py:487
  149.6 10.0 %collective-permute-done.1.refs_2_ = bf16[192,512]{1,0:T(8,128)(2,1)S(1)} collective-permute-done((bf16[192,512]{1,0:T(8,128)(2,1)}, bf16[192,512]{1,0:T(8,128)(2,1)S(1)}, u32[]{:S(2)}, u32[]{:S(2)}) %collective-permute-start.1) | collective-permute-done | bytes 196640 | tf_op jit(solution)/shard_map/ppermute | solution.py:97
  197.5 25.8 %collective-permute-done.26.refs_4_ = bf16[192,2560]{1,0:T(8,128)(2,1)} collective-permute-done((bf16[192,2560]{1,0:T(8,128)(2,1)}, bf16[192,2560]{1,0:T(8,128)(2,1)}, u32[]{:S(2)}, u32[]{:S(2)}) %collective-permute-start.26) | collective-permute-done | bytes 983072 | tf_op jit(solution)/shard_map/ppermute | solution.py:97
  226.2 22.5 %collective-permute-done.28.refs_6_ = bf16[96,2560]{1,0:T(8,128)(2,1)S(1)} collective-permute-done((bf16[96,2560]{1,0:T(8,128)(2,1)S(1)}, bf16[96,2560]{1,0:T(8,128)(2,1)S(1)}, u32[]{:S(2)}, u32[]{:S(2)}) %collective-permute-start.28) | collective-permute-done | bytes 491552 | tf_op jit(solution)/shard_map/ppermute | solution.py:97
  263.4 33.0 %collective-permute-done.32.refs_0_ = bf16[8,80,512]{2,1,0:T(8,128)(2,1)S(1)} collective-permute-done((bf16[8,80,512]{2,1,0:T(8,128)(2,1)S(1)}, bf16[8,80,512]{2,1,0:T(8,128)(2,1)S(1)}, u32[]{:S(2)}, u32[]{:S(2)}) %collective-permute-start.32) | collective-permute-done | bytes 655392 | tf_op jit(solution)/shard_map/ppermute | solution.py:103
  323.4 7.6 %gather_blocks.5 = bf16[8,192,2560]{2,1,0:T(8,128)(2,1)} custom-call(s32[10]{0:T(128)} %stack.101.places_ref, bf16[192,2560]{1,0:T(8,128)(2,1)} %reorder.4.refs_0_.refs_4_, bf16[192,2560]{1,0:T(8,128)(2,1)} %copy-done.22, bf16[192,2560]{1,0:T(8,128)(2,1)} %copy-done.16, bf16[192,2560]{1,0:T(8,128)(2,1)} %copy-done.23, ...), custom_call_target="tpu_custom_call" | custom-call | bytes 15728640 | tf_op jit(solution)/shard_map/gather_blocks/pallas_call | solution.py:136
  331.1 25.7 %collective-permute-done.34.refs_2_ = bf16[8,80,512]{2,1,0:T(8,128)(2,1)} collective-permute-done((bf16[8,80,512]{2,1,0:T(8,128)(2,1)}, bf16[8,80,512]{2,1,0:T(8,128)(2,1)}, u32[]{:S(2)}, u32[]{:S(2)}) %collective-permute-start.34) | collective-permute-done | bytes 655392 | tf_op jit(solution)/shard_map/ppermute | solution.py:103
  363.5 9.5 %row_product.1 = f32[1536,512]{1,0:T(8,128)} custom-call(bf16[1536,2560]{1,0:T(8,128)(2,1)} %bitcast.136, bf16[2560,512]{1,0:T(8,128)(2,1)} %bitcast.148), custom_call_target="tpu_custom_call" | custom-call | flops 4026531840 | bytes 13631488 | tf_op jit(solution)/shard_map/row_product/pallas_call | solution.py:783
  379.2 24.3 %feed_forward.1 = (bf16[4,2,192,512]{3,2,1,0:T(8,128)(2,1)}, bf16[4,2,192,1024]{3,2,1,0:T(8,128)(2,1)}, bf16[768,2560]{1,0:T(8,128)(2,1)}, bf16[768,2560]{1,0:T(8,128)(2,1)}) custom-call(s32[1]{0:T(128)} %bitcast.19.core_ref, bf16[4,2,192,2560]{3,2,1,0:T(8,128)(2,1)} %bitcast.171, bf16[2560,1024]{1,0:T(8,128)(2,1)} %bitcast.139, f32[4,2,192,512]{3,2,1,0:T(8,128)} %bitcast.174), custom_call_target="tpu_custom_call" | custom-call | flops 16106127360 | bytes 28835840 | tf_op jit(solution)/shard_map/feed_forward/pallas_call | solution.py:748
  403.5 12.5 %weight_term.3 = bf16[4,4,2,80,1024]{4,3,2,1,0:T(8,128)(2,1)} custom-call(bf16[1536,2560]{1,0:T(8,128)(2,1)} %all-gather.8.cloned.1.call-done.left_ref, bf16[1536,1024]{1,0:T(8,128)(2,1)} %bitcast.175), custom_call_target="tpu_custom_call" | custom-call | flops 8053063680 | bytes 16252928 | tf_op jit(solution)/shard_map/weight_term/pallas_call | solution.py:906
  426.0 9.6 %down_product.1 = (bf16[768,2560]{1,0:T(8,128)(2,1)}, bf16[768,2560]{1,0:T(8,128)(2,1)}) custom-call(s32[1]{0:T(128)} %bitcast.19.core_ref, bf16[4,2,192,512]{3,2,1,0:T(8,128)(2,1)} %get-tuple-element.56.in_ref, bf16[2560,512]{1,0:T(8,128)(2,1)} %bitcast.149), custom_call_target="tpu_custom_call" | custom-call | flops 4026531840 | bytes 12058624 | tf_op jit(solution)/shard_map/down_product/pallas_call | solution.py:870
  437.5 10.1 %collective-permute-done.46 = bf16[2,96,2560]{2,1,0:T(8,128)(2,1)} collective-permute-done((bf16[2,96,2560]{2,1,0:T(8,128)(2,1)}, bf16[2,96,2560]{2,1,0:T(8,128)(2,1)}, u32[]{:S(2)}, u32[]{:S(2)}) %collective-permute-start.46) | collective-permute-done | bytes 983072 | tf_op jit(solution)/shard_map/ppermute | solution.py:97
  450.5 10.0 %collective-permute-done.44 = bf16[2,96,2560]{2,1,0:T(8,128)(2,1)S(1)} collective-permute-done((bf16[2,96,2560]{2,1,0:T(8,128)(2,1)S(1)}, bf16[2,96,2560]{2,1,0:T(8,128)(2,1)S(1)}, u32[]{:S(2)}, u32[]{:S(2)}) %collective-permute-start.44) | collective-permute-done | bytes 983072 | tf_op jit(solution)/shard_map/ppermute | solution.py:97
  483.9 8.8 %attend_back.1 = (bf16[192,1280]{1,0:T(8,128)(2,1)}, f32[768,512]{1,0:T(8,128)}, bf16[768,512]{1,0:T(8,128)(2,1)}) custom-call(bf16[192,512]{1,0:T(8,128)(2,1)} %pad_maximum_fusion.refs_0_, bf16[192,512]{1,0:T(8,128)(2,1)} %collective-permute-done.refs_1_, bf16[192,512]{1,0:T(8,128)(2,1)} %copy-done.51, bf16[192,512]{1,0:T(8,128)(2,1)} %copy-done.52, ...), custom_call_target="tpu_custom_call" | custom-call | flops 3774873600 | bytes 5210112 | tf_op jit(solution)/shard_map/attend_back/pallas_call | solution.py:679
  502.7 13.1 %collective-permute-done.49.refs_0_ = bf16[192,512]{1,0:T(8,128)(2,1)S(1)} collective-permute-done((bf16[192,512]{1,0:T(8,128)(2,1)S(1)}, bf16[192,512]{1,0:T(8,128)(2,1)S(1)}, u32[]{:S(2)}, u32[]{:S(2)}) %collective-permute-start.49) | collective-permute-done | bytes 196640 | tf_op jit(solution)/shard_map/ppermute | solution.py:97
  531.6 8.6 %weight_term.2 = bf16[4,4,2,80,512]{4,3,2,1,0:T(8,128)(2,1)} custom-call(bf16[1536,2560]{1,0:T(8,128)(2,1)} %bitcast.137, bf16[1536,512]{1,0:T(8,128)(2,1)} %bitcast.176), custom_call_target="tpu_custom_call" | custom-call | flops 4026531840 | bytes 12058624 | tf_op jit(solution)/shard_map/weight_term/pallas_call | solution.py:906
  557.4 14.1 %collective-permute-done.39.refs_1_ = bf16[2,96,2560]{2,1,0:T(8,128)(2,1)} collective-permute-done((bf16[2,96,2560]{2,1,0:T(8,128)(2,1)}, bf16[2,96,2560]{2,1,0:T(8,128)(2,1)}, u32[]{:S(2)}, u32[]{:S(2)}) %collective-permute-start.39) | collective-permute-done | bytes 983072 | tf_op jit(solution)/shard_map/ppermute | solution.py:97
  598.7 8.3 %collective-permute-done.60 = bf16[2,160,1280]{2,1,0:T(8,128)(2,1)} collective-permute-done((bf16[2,160,1280]{2,1,0:T(8,128)(2,1)}, bf16[2,160,1280]{2,1,0:T(8,128)(2,1)}, u32[]{:S(2)}, u32[]{:S(2)}) %collective-permute-start.60) | collective-permute-done | bytes 819232 | tf_op jit(solution)/shard_map/ppermute | solution.py:97
  621.5 10.4 %collective-permute-done.53.refs_1_ = bf16[2,160,1280]{2,1,0:T(8,128)(2,1)S(1)} collective-permute-done((bf16[2,160,1280]{2,1,0:T(8,128)(2,1)}, bf16[2,160,1280]{2,1,0:T(8,128)(2,1)S(1)}, u32[]{:S(2)}, u32[]{:S(2)}) %collective-permute-start.53) | collective-permute-done | bytes 819232 | tf_op jit(solution)/shard_map/ppermute | solution.py:97
  683.6 10.6 %input_grads.1 = f32[192,2560]{1,0:T(8,128)} custom-call(bf16[192,1280]{1,0:T(8,128)(2,1)} %get-tuple-element.72.dq_ref, bf16[192,512]{1,0:T(8,128)(2,1)} %key_value_grads.1.dkv_ref, bf16[2560,1920]{1,0:T(8,128)(2,1)} %all-gather.6.cloned.1.call-done.weight_ref, f32[192,2560]{1,0:T(8,128)} %get-tuple-element.75.grad_ref, ...), custom_call_target="tpu_custom_call" | custom-call | flops 1761607680 | bytes 14745600 | tf_op jit(solution)/shard_map/input_grads/pallas_call | solution.py:838
  694.2 10.4 %collective-permute-done.67.refs_1_ = bf16[80,3072]{1,0:T(8,128)(2,1)S(1)} collective-permute-done((bf16[80,3072]{1,0:T(8,128)(2,1)}, bf16[80,3072]{1,0:T(8,128)(2,1)S(1)}, u32[]{:S(2)}, u32[]{:S(2)}) %collective-permute-start.67) | collective-permute-done | bytes 491552 | tf_op jit(solution)/shard_map/ppermute | solution.py:97
  (353 shorter events, 338.8 us)
Async XLA Ops:
  9.7 122.2 %all-gather.6.cloned.1.call-start = ((), (), s32[]{:S(2)}) async-start(), calls=%async_computation.6 | async-start | bytes 11059200 | tf_op jit(solution)/shard_map/all_gather | solution.py:84
  42.3 337.0 %all-gather.8.cloned.1.call-start = ((), (), s32[]{:S(2)}) async-start(), calls=%async_computation.7 | async-start | bytes 8847360 | tf_op jit(solution)/shard_map/all_gather | solution.py:84
  69.1 62.8 %collective-permute-start.15 = (bf16[320,1280]{1,0:T(8,128)(2,1)}, bf16[320,1280]{1,0:T(8,128)(2,1)}, u32[]{:S(2)}, u32[]{:S(2)}) collective-permute-start(bf16[320,1280]{1,0:T(8,128)(2,1)} %bitcast.143), channel_id=1, source_target_pairs={{0,24},{8,16},{16,8},{24,0},{1,25},{9,17},{17,9},{25,1},{2,26},{10... | collective-permute-start | bytes 2457608 | tf_op jit(solution)/shard_map/ppermute | solution.py:487
  74.2 67.3 %collective-permute-start.10 = (bf16[320,1280]{1,0:T(8,128)(2,1)S(1)}, bf16[320,1280]{1,0:T(8,128)(2,1)}, u32[]{:S(2)}, u32[]{:S(2)}) collective-permute-start(bf16[320,1280]{1,0:T(8,128)(2,1)S(1)} %bitcast.145), channel_id=1, source_target_pairs={{0,1},{1,0},{2,3},{3,2},{4,5},{5,4},{6,7},{7,6},{8,9},{9,8},{10,11... | collective-permute-start | bytes 2457608 | tf_op jit(solution)/shard_map/ppermute | solution.py:97
  99.0 44.3 %collective-permute-start.12 = (bf16[320,1280]{1,0:T(8,128)(2,1)S(1)}, bf16[320,1280]{1,0:T(8,128)(2,1)}, u32[]{:S(2)}, u32[]{:S(2)}) collective-permute-start(bf16[320,1280]{1,0:T(8,128)(2,1)S(1)} %collective-permute-done.11.refs_2_), channel_id=1, source_target_pairs={{0,1},{1,0},{2,3},{3,2},{4,5},{5,4},{6,7},{7,6},{8,9},{9,8},{10,11... | collective-permute-start | bytes 2457608 | tf_op jit(solution)/shard_map/ppermute | solution.py:97
  102.0 42.5 %collective-permute-start.14 = (bf16[320,1280]{1,0:T(8,128)(2,1)S(1)}, bf16[320,1280]{1,0:T(8,128)(2,1)}, u32[]{:S(2)}, u32[]{:S(2)}) collective-permute-start(bf16[320,1280]{1,0:T(8,128)(2,1)S(1)} %collective-permute-done.13.refs_4_), channel_id=1, source_target_pairs={{0,1},{1,0},{2,3},{3,2},{4,5},{5,4},{6,7},{7,6},{8,9},{9,8},{10,11... | collective-permute-start | bytes 2457608 | tf_op jit(solution)/shard_map/ppermute | solution.py:97
  184.1 427.0 %reduce-scatter.5.cloned.1.call-start = ((), (), s32[]{:S(2)}) async-start(), calls=%async_computation.9 | async-start | bytes 6553600 | tf_op jit(solution)/shard_map/reduce_scatter | solution.py:88
  191.4 57.9 %collective-permute-start.17 = (bf16[8,80,1024]{2,1,0:T(8,128)(2,1)S(1)}, bf16[8,80,1024]{2,1,0:T(8,128)(2,1)S(1)}, u32[]{:S(2)}, u32[]{:S(2)}) collective-permute-start(bf16[8,80,1024]{2,1,0:T(8,128)(2,1)S(1)} %slice.77.mine_ref), channel_id=1, source_target_pairs={{0,2},{2,4},{4,6},{1,3},{3,5},{5,7},{8,10},{10,12},{12,14},{9,11},... | collective-permute-start | bytes 3932168 | tf_op jit(solution)/shard_map/ppermute | solution.py:103
  193.4 57.9 %collective-permute-start.20 = (bf16[8,80,1024]{2,1,0:T(8,128)(2,1)S(1)}, bf16[8,80,1024]{2,1,0:T(8,128)(2,1)S(1)}, u32[]{:S(2)}, u32[]{:S(2)}) collective-permute-start(bf16[8,80,1024]{2,1,0:T(8,128)(2,1)S(1)} %slice.77.mine_ref), channel_id=1, source_target_pairs={{2,0},{4,2},{6,4},{3,1},{5,3},{7,5},{10,8},{12,10},{14,12},{11,9},... | collective-permute-start | bytes 3932168 | tf_op jit(solution)/shard_map/ppermute | solution.py:103
  197.4 60.0 %collective-permute-start.23 = (bf16[192,2560]{1,0:T(8,128)(2,1)S(1)}, bf16[192,2560]{1,0:T(8,128)(2,1)S(1)}, u32[]{:S(2)}, u32[]{:S(2)}) collective-permute-start(bf16[192,2560]{1,0:T(8,128)(2,1)S(1)} %copy-done.4), channel_id=1, source_target_pairs={{0,1},{1,0},{2,3},{3,2},{4,5},{5,4},{6,7},{7,6},{8,9},{9,8},{10,11... | collective-permute-start | bytes 2949128 | tf_op jit(solution)/shard_map/ppermute | solution.py:97
  249.3 53.9 %collective-permute-start.18 = (bf16[8,80,1024]{2,1,0:T(8,128)(2,1)S(1)}, bf16[8,80,1024]{2,1,0:T(8,128)(2,1)}, u32[]{:S(2)}, u32[]{:S(2)}) collective-permute-start(bf16[8,80,1024]{2,1,0:T(8,128)(2,1)S(1)} %collective-permute-done.17.refs_0_), channel_id=1, source_target_pairs={{0,2},{2,4},{4,6},{1,3},{3,5},{5,7},{8,10},{10,12},{12,14},{9,11},... | collective-permute-start | bytes 3932168 | tf_op jit(solution)/shard_map/ppermute | solution.py:103
  251.3 53.9 %collective-permute-start.21 = (bf16[8,80,1024]{2,1,0:T(8,128)(2,1)S(1)}, bf16[8,80,1024]{2,1,0:T(8,128)(2,1)}, u32[]{:S(2)}, u32[]{:S(2)}) collective-permute-start(bf16[8,80,1024]{2,1,0:T(8,128)(2,1)S(1)} %collective-permute-done.20.refs_3_), channel_id=1, source_target_pairs={{2,0},{4,2},{6,4},{3,1},{5,3},{7,5},{10,8},{12,10},{14,12},{11,9},... | collective-permute-start | bytes 3932168 | tf_op jit(solution)/shard_map/ppermute | solution.py:103
  257.4 45.8 %collective-permute-start.25 = (bf16[192,2560]{1,0:T(8,128)(2,1)S(1)}, bf16[192,2560]{1,0:T(8,128)(2,1)S(1)}, u32[]{:S(2)}, u32[]{:S(2)}) collective-permute-start(bf16[192,2560]{1,0:T(8,128)(2,1)S(1)} %collective-permute-done.24.refs_2_), channel_id=1, source_target_pairs={{0,1},{1,0},{2,3},{3,2},{4,5},{5,4},{6,7},{7,6},{8,9},{9,8},{10,11... | collective-permute-start | bytes 2949128 | tf_op jit(solution)/shard_map/ppermute | solution.py:97
  259.4 39.2 %collective-permute-start.35 = (bf16[8,80,512]{2,1,0:T(8,128)(2,1)S(1)}, bf16[8,80,512]{2,1,0:T(8,128)(2,1)S(1)}, u32[]{:S(2)}, u32[]{:S(2)}) collective-permute-start(bf16[8,80,512]{2,1,0:T(8,128)(2,1)S(1)} %slice.80.mine_ref), channel_id=1, source_target_pairs={{2,0},{4,2},{6,4},{3,1},{5,3},{7,5},{10,8},{12,10},{14,12},{11,9},... | collective-permute-start | bytes 1966088 | tf_op jit(solution)/shard_map/ppermute | solution.py:103
  303.3 69.8 %collective-permute-start.19 = (bf16[8,80,1024]{2,1,0:T(8,128)(2,1)}, bf16[8,80,1024]{2,1,0:T(8,128)(2,1)}, u32[]{:S(2)}, u32[]{:S(2)}) collective-permute-start(bf16[8,80,1024]{2,1,0:T(8,128)(2,1)} %collective-permute-done.18.refs_1_), channel_id=1, source_target_pairs={{0,2},{2,4},{4,6},{1,3},{3,5},{5,7},{8,10},{10,12},{12,14},{9,11},... | collective-permute-start | bytes 3932168 | tf_op jit(solution)/shard_map/ppermute | solution.py:103
  305.2 67.8 %collective-permute-start.22 = (bf16[8,80,1024]{2,1,0:T(8,128)(2,1)}, bf16[8,80,1024]{2,1,0:T(8,128)(2,1)}, u32[]{:S(2)}, u32[]{:S(2)}) collective-permute-start(bf16[8,80,1024]{2,1,0:T(8,128)(2,1)} %collective-permute-done.21.refs_4_), channel_id=1, source_target_pairs={{2,0},{4,2},{6,4},{3,1},{5,3},{7,5},{10,8},{12,10},{14,12},{11,9},... | collective-permute-start | bytes 3932168 | tf_op jit(solution)/shard_map/ppermute | solution.py:103
  316.0 40.8 %collective-permute-start.34 = (bf16[8,80,512]{2,1,0:T(8,128)(2,1)}, bf16[8,80,512]{2,1,0:T(8,128)(2,1)}, u32[]{:S(2)}, u32[]{:S(2)}) collective-permute-start(bf16[8,80,512]{2,1,0:T(8,128)(2,1)} %collective-permute-done.33.refs_1_), channel_id=1, source_target_pairs={{0,2},{2,4},{4,6},{1,3},{3,5},{5,7},{8,10},{10,12},{12,14},{9,11},... | collective-permute-start | bytes 1966088 | tf_op jit(solution)/shard_map/ppermute | solution.py:103
  318.3 40.8 %collective-permute-start.37 = (bf16[8,80,512]{2,1,0:T(8,128)(2,1)}, bf16[8,80,512]{2,1,0:T(8,128)(2,1)}, u32[]{:S(2)}, u32[]{:S(2)}) collective-permute-start(bf16[8,80,512]{2,1,0:T(8,128)(2,1)} %collective-permute-done.36.refs_4_), channel_id=1, source_target_pairs={{2,0},{4,2},{6,4},{3,1},{5,3},{7,5},{10,8},{12,10},{14,12},{11,9},... | collective-permute-start | bytes 1966088 | tf_op jit(solution)/shard_map/ppermute | solution.py:103
  416.1 225.0 %reduce-scatter.3.cloned.1.call-start = ((), (), s32[]{:S(2)}) async-start(), calls=%async_computation.8 | async-start | bytes 3276800 | tf_op jit(solution)/shard_map/reduce_scatter | solution.py:88
  435.5 104.7 %collective-permute-start.38 = (bf16[2,2,192,2560]{3,2,1,0:T(8,128)(2,1)}, bf16[2,2,192,2560]{3,2,1,0:T(8,128)(2,1)}, u32[]{:S(2)}, u32[]{:S(2)}) collective-permute-start(bf16[2,2,192,2560]{3,2,1,0:T(8,128)(2,1)} %bitcast.172), channel_id=1, source_target_pairs={{0,1},{1,0},{2,3},{3,2},{4,5},{5,4},{6,7},{7,6},{8,9},{9,8},{10,11... | collective-permute-start | bytes 11796488 | tf_op jit(solution)/shard_map/ppermute | solution.py:97
  501.9 78.6 %collective-permute-start.57 = (bf16[2,2,320,1280]{3,2,1,0:T(8,128)(2,1)}, bf16[2,2,320,1280]{3,2,1,0:T(8,128)(2,1)}, u32[]{:S(2)}, u32[]{:S(2)}) collective-permute-start(bf16[2,2,320,1280]{3,2,1,0:T(8,128)(2,1)} %dynamic-slice_bitcast_fusion), channel_id=1, source_target_pairs={{0,1},{1,0},{2,3},{3,2},{4,5},{5,4},{6,7},{7,6},{8,9},{9,8},{10,11... | collective-permute-start | bytes 9830408 | tf_op jit(solution)/shard_map/ppermute | solution.py:97
  590.9 47.3 %collective-permute-start.66 = (bf16[160,512]{1,0:T(8,128)(2,1)}, bf16[160,512]{1,0:T(8,128)(2,1)S(1)}, u32[]{:S(2)}, u32[]{:S(2)}) collective-permute-start(bf16[160,512]{1,0:T(8,128)(2,1)} %fusion.15), channel_id=1, source_target_pairs={{0,8},{8,0},{1,9},{9,1},{2,10},{10,2},{3,11},{11,3},{4,12},{12,4},... | collective-permute-start | bytes 491528 | tf_op jit(solution)/shard_map/ppermute | solution.py:97
  592.2 57.4 %collective-permute-start.64 = (bf16[160,512]{1,0:T(8,128)(2,1)}, bf16[160,512]{1,0:T(8,128)(2,1)}, u32[]{:S(2)}, u32[]{:S(2)}) collective-permute-start(bf16[160,512]{1,0:T(8,128)(2,1)} %fusion.14), channel_id=1, source_target_pairs={{0,16},{16,0},{1,17},{17,1},{2,18},{18,2},{3,19},{19,3},{4,20},{20... | collective-permute-start | bytes 491528 | tf_op jit(solution)/shard_map/ppermute | solution.py:97
  646.0 77.9 %all-to-all-start.2 = ((bf16[8,80,512]{2,1,0:T(8,128)(2,1)}), bf16[8,80,512]{2,1,0:T(8,128)(2,1)S(1)}, u32[]{:S(2)}, u32[]{:S(2)}) async-start(bf16[8,80,512]{2,1,0:T(8,128)(2,1)} %bitcast.162), calls=%async_computation.4 | async-start | bytes 1310720 | tf_op jit(solution)/shard_map/all_to_all | solution.py:92
  (110 other events, 2308.2 us)
Sparse Core Ops, SparseCore 0:
  10.1 31.9 all-gather.3
  43.9 86.3 all-gather.5
  184.1 73.9 all-gather.7
  416.2 106.1 reduce-scatter.4
  540.4 52.9 reduce-scatter.2
